TPU v7x, 32 devices: a whole 2x2x4 slice. The times are simulated.
32 devices in a mesh: row: 8 (over z, x), col: 4 (over y, core).
Axes of the slice: x: 2, y: 2, z: 4, core: 2. Of those that a mesh axis runs over, the one named last changes fastest.
Arguments:
- gram_tiles: float32 [2, 8, 4, 4, 512, 512], P(None, 'row', None, 'col'), as said below
Outputs:
- factor_tiles: float32 [2, 8, 4, 4, 512, 512], P(None, 'row', None, 'col')
Inputs may be any that keep to these rules, and one draw needn't show every extreme that they name: gram_tiles holds a symmetric positive definite matrix with positive entries.
All inputs are finite; a program needn't handle non-finite values.
Results may differ from a plain program's by a relative error of at most 0.0001.
Values sent between devices are 32-bit elements; how exact they have to be, the bound alone decides.
No kernel may reach another device: no remote copies, remote signals or barrier semaphores. Data moves between devices by JAX's collectives and lax.ppermute only.
A program may use at most 128 MiB of HBM per device.

v0:
```python
import functools

import jax
import jax.numpy as jnp
from jax import lax
from jax.experimental import pallas as pl
from jax.experimental.pallas import tpu as pltpu
from jax.sharding import PartitionSpec as P

GROUP = 8
BLOCK = 128
AXES = ("row", "y", "core")


def contract(a, b, ca, cb, precision=lax.Precision.HIGHEST):
    return lax.dot_general(
        a, b, (((ca,), (cb,)), ((), ())), precision=precision, preferred_element_type=jnp.float32
    )


def factor_block(s_ref, e_ref, u_ref):
    n = s_ref.shape[0]
    sub = lax.broadcasted_iota(jnp.int32, (GROUP, n), 0)
    lane = lax.broadcasted_iota(jnp.int32, (GROUP, n), 1)
    down = lax.broadcasted_iota(jnp.int32, (n, n), 0)
    across = lax.broadcasted_iota(jnp.int32, (n, n), 1)
    e_ref[...] = (down == across).astype(jnp.float32)
    for start in range(0, n, GROUP):
        stop = start + GROUP
        tall = s_ref[start:stop, :]
        unit = e_ref[start:stop, :]
        entry = {}
        for j in range(GROUP):
            for i in range(j, GROUP):
                entry[i, j] = jnp.broadcast_to(tall[j : j + 1, start + i : start + i + 1], (1, n))
        rows = [tall[t : t + 1, :] for t in range(GROUP)]
        units = [unit[t : t + 1, :] for t in range(GROUP)]
        for t in range(GROUP):
            scale = lax.rsqrt(entry[t, t])
            for i in range(t + 1, GROUP):
                entry[i, t] = entry[i, t] * scale
            rows[t] = rows[t] * scale
            units[t] = units[t] * scale
            for i in range(t + 1, GROUP):
                for j in range(t + 1, i + 1):
                    entry[i, j] = entry[i, j] - entry[i, t] * entry[j, t]
                rows[i] = rows[i] - entry[i, t] * rows[t]
                units[i] = units[i] - entry[i, t] * units[t]
        u = jnp.where(lane >= sub + start, jnp.concatenate(rows, 0), 0.0)
        v = jnp.concatenate(units, 0)
        u_ref[start:stop, :] = u
        e_ref[start:stop, :] = v
        if stop < n:
            s_ref[stop:, :] = s_ref[stop:, :] - contract(u, u, 0, 0)[stop:, :]
            e_ref[stop:, :] = e_ref[stop:, :] - contract(u, v, 0, 0)[stop:, :]


def eliminate(first, last, a_ref, l_ref, w_ref, s_ref, e_ref, u_ref):
    def step(k):
        begin = k * BLOCK
        end = begin + BLOCK
        at = slice(begin, end)
        later = slice(end, a_ref.shape[0])
        inverse = e_ref[...]
        l_ref[at, at] = u_ref[...].T
        w_ref[at, at] = inverse
        if begin > 0:
            solved = contract(inverse, w_ref[at, :begin], 1, 0)
            w_ref[at, :begin] = solved
        if end < a_ref.shape[0]:
            below = contract(a_ref[later, at], inverse, 1, 1)
            l_ref[later, at] = below
            a_ref[later, later] -= contract(below, below, 1, 1)
            w_ref[later, at] = -contract(below, inverse, 1, 0)
            if begin > 0:
                w_ref[later, :begin] -= contract(below, solved, 1, 0)

    def body(k, carry):
        at = pl.ds(pl.multiple_of(k * BLOCK, BLOCK), BLOCK)
        s_ref[...] = a_ref[at, at]
        factor_block(s_ref, e_ref, u_ref)
        for known in range(first, last):

            @pl.when(k == known)
            def _():
                step(known)

        return carry

    lax.fori_loop(first, last, body, 0)


def open_kernel(last, x_ref, rest_ref, l_ref, w_ref, a_ref, *scratch):
    a_ref[...] = x_ref[...]
    l_ref[...] = jnp.zeros_like(l_ref)
    w_ref[...] = jnp.zeros_like(w_ref)
    eliminate(0, last, a_ref, l_ref, w_ref, *scratch)
    rest_ref[...] = a_ref[last * BLOCK :, last * BLOCK :]


def corner_kernel(last, side_ref, x_ref, inverse_ref, p_ref, rest_ref, l_ref, w_ref, a_ref, *scratch):
    n = x_ref.shape[0]
    half = n // 2

    def solve(c, carry):
        at = pl.ds(pl.multiple_of(c * half, half), half)
        p_ref[:, at] = contract(side_ref[...], inverse_ref[at, :], 1, 1)
        return carry

    def subtract(c, carry):
        at = pl.ds(pl.multiple_of(c * half, half), half)
        a_ref[:, at] = x_ref[:, at] - contract(p_ref[...], p_ref[at, :], 1, 1)
        return carry

    lax.fori_loop(0, 2, solve, 0)
    lax.fori_loop(0, 2, subtract, 0)
    l_ref[...] = jnp.zeros_like(l_ref)
    w_ref[...] = jnp.zeros_like(w_ref)
    eliminate(0, last, a_ref, l_ref, w_ref, *scratch)
    rest_ref[...] = a_ref[last * BLOCK :, last * BLOCK :]


def close_kernel(first, last, rest_ref, l_in, w_in, l_ref, w_ref, a_ref, *scratch):
    a_ref[first * BLOCK :, first * BLOCK :] = rest_ref[...]
    l_ref[...] = l_in[...]
    w_ref[...] = w_in[...]
    eliminate(first, last, a_ref, l_ref, w_ref, *scratch)


def call(kernel, n, inputs, outputs):
    small = pltpu.VMEM((BLOCK, BLOCK), jnp.float32)
    space = pl.BlockSpec(memory_space=pltpu.VMEM)
    return pl.pallas_call(
        kernel,
        out_shape=[jax.ShapeDtypeStruct((size, size), jnp.float32) for size in outputs],
        in_specs=[space] * len(inputs),
        out_specs=[space] * len(outputs),
        scratch_shapes=[pltpu.VMEM((n, n), jnp.float32), small, small, small],
        cost_estimate=pl.CostEstimate(flops=20_000_000_000, bytes_accessed=60_000_000, transcendentals=0),
    )(*inputs)


def halfway(n):
    return n // BLOCK // 2


def left(n):
    return n - halfway(n) * BLOCK


def factor_open(x):
    n = x.shape[0]
    return call(functools.partial(open_kernel, halfway(n)), n, (x,), (left(n), n, n))


def factor_corner(side, x, inverse):
    n = x.shape[0]
    return call(functools.partial(corner_kernel, halfway(n)), n, (side, x, inverse), (n, left(n), n, n))


def factor_close(rest, l, w):
    n = l.shape[0]
    return call(functools.partial(close_kernel, halfway(n), n // BLOCK), n, (rest, l, w), (n, n))


class Grid:
    def __init__(self):
        self.rows = lax.axis_size("row")
        self.ys = lax.axis_size("y")
        self.cols = self.ys * 2
        self.his = self.rows // 2
        self.row, self.y, self.core = [lax.axis_index(axis) for axis in AXES]
        self.col = self.y * 2 + self.core
        self.hi, self.lo = self.row // 2, self.row % 2

    def send(self, x, target):
        pairs = []
        for hi in range(self.his):
            for lo in range(2):
                for y in range(self.ys):
                    for core in range(2):
                        to = target(hi, lo, y, core)
                        if to is not None:
                            pairs.append((self.number(hi, lo, y, core), self.number(*to)))
        return lax.ppermute(x, AXES, pairs)

    def number(self, hi, lo, y, core):
        return (hi * 2 + lo) * self.cols + y * 2 + core

    def swap_lo(self, x):
        return self.send(x, lambda hi, lo, y, core: (hi, 1 - lo, y, core))

    def swap_core(self, x):
        return self.send(x, lambda hi, lo, y, core: (hi, lo, y, 1 - core))

    def swap_y(self, x, s):
        return self.send(x, lambda hi, lo, y, core: (hi, lo, y ^ s, core))

    def swap_hi(self, x, s):
        return self.send(x, lambda hi, lo, y, core: (hi ^ s, lo, y, core))


def after(x, *values):
    return lax.optimization_barrier((x, *values))[0]


def order_blocks(n):
    count = n // BLOCK
    lower = [(i, j) for i in range(count) for j in range(i + 1)]
    return lower, [(i, j) for i in range(count) for j in range(i + 1, count)]


def join(n, lookup):
    count = n // BLOCK
    zero = jnp.zeros((BLOCK, BLOCK), jnp.float32)
    return jnp.concatenate(
        [jnp.concatenate([lookup.get((i, j), zero) for j in range(count)], 1) for i in range(count)], 0
    )


def scatter(grid, tile):
    n = tile.shape[0]
    total = grid.rows * grid.cols
    parts = []
    for at in order_blocks(n):
        blocks = [tile[i * BLOCK : (i + 1) * BLOCK, j * BLOCK : (j + 1) * BLOCK] for i, j in at]
        parts.append(jnp.stack(blocks).reshape(total, -1, BLOCK))
    lower = parts[0].shape[1]
    got = lax.all_to_all(jnp.concatenate(parts, 1), AXES, 0, 0, tiled=True)
    corner, side, last = got[0, :lower], got[grid.cols], got[grid.cols + 1, :lower]
    return corner, jnp.concatenate([side, last], 0)


def gather(grid, part):
    spread = jnp.broadcast_to(part[None], (grid.rows * grid.ys, *part.shape))
    mine = lax.all_to_all(spread, ("row", "y"), 0, 0, tiled=True)
    return mine, grid.swap_core(mine)


def merge(grid, mine, other):
    even = grid.core == 0
    whole = jnp.stack([jnp.where(even, mine, other), jnp.where(even, other, mine)], 1)
    return whole.reshape(-1, *mine.shape[1:])


def unpack_lower(n, packed):
    lower, _ = order_blocks(n)
    packed = packed.reshape(len(lower), BLOCK, BLOCK)
    return join(n, {key: packed[k] for k, key in enumerate(lower)})


def unpack_sides(n, packed):
    lower, upper = order_blocks(n)
    rows = len(lower) * BLOCK // packed.shape[0]
    more = rows + len(upper) * BLOCK // packed.shape[0]
    low = packed[:, :rows].reshape(len(lower), BLOCK, BLOCK)
    high = packed[:, rows:more].reshape(len(upper), BLOCK, BLOCK)
    lookup = {key: low[k] for k, key in enumerate(lower)}
    lookup.update({key: high[k] for k, key in enumerate(upper)})
    return join(n, lookup), unpack_lower(n, packed[:, more:])


def split(x):
    high = x.astype(jnp.bfloat16)
    return high, (x - high.astype(jnp.float32)).astype(jnp.bfloat16)


def product(a, b, cb):
    def one(x, y):
        return lax.dot_general(x, y, (((1,), (cb,)), ((), ())), preferred_element_type=jnp.float32)

    return one(a[0], b[0]) + (one(a[0], b[1]) + one(a[1], b[0]))


def finish_kernel(shape, steps, opening, scalars, *refs):
    count, width, n = shape
    extra = count if opening else 0
    total = extra + len(steps)
    g_ref, l0_ref, l10_ref, l1_ref, w0_ref, w1_ref = refs[:6]
    refs = refs[6:]
    own = refs[: 2 * extra]
    refs = refs[2 * extra :]
    sets = [refs[4 * e : 4 * e + 4] for e in range(len(steps))]
    refs = refs[4 * len(steps) :]
    if not opening:
        _, rows_in = refs[0], refs[1:3]
        refs = refs[3:]
    out_ref = refs[0]
    rows_out = refs[1:3] if opening else ()
    refs = refs[3:] if opening else refs[1:]
    raw, high, low, keep, w0h, w0l, w1h, w1l, lh, ll, gbuf, obuf, rsem, gsem, osem, psem = refs
    core, same_lo, half, row0, row1, col = [scalars[k] for k in range(6)]

    def fetch(condition, ref, slot, panel):
        @pl.when(condition)
        def _():
            pltpu.make_async_copy(ref, raw.at[slot, panel], rsem.at[slot, panel]).start()

    for panel in range(2):
        for a in range(extra):
            fetch(core == panel, own[a], a, panel)
            fetch(core != panel, own[extra + a], a, panel)
    for e in range(len(steps)):
        straight, straight_got, crossed, crossed_got = sets[e]
        for panel in range(2):
            fetch((same_lo == 1) & (core == panel), straight, extra + e, panel)
            fetch((same_lo == 1) & (core != panel), straight_got, extra + e, panel)
            fetch((same_lo == 0) & (core == panel), crossed, extra + e, panel)
            fetch((same_lo == 0) & (core != panel), crossed_got, extra + e, panel)

    def column(e):
        slot = far = 0
        for at, (s, f) in enumerate(steps):
            slot = jnp.where(e == at, s, slot)
            far = jnp.where(e == at, f, far)
        return 2 * slot + jnp.where(far == 1, 1 - half, half)

    def place(k):
        return lax.rem(k, count), column(k // count)

    def g_copy(k, slot):
        a, t = place(k)
        return pltpu.make_async_copy(g_ref.at[a, t], gbuf.at[slot], gsem.at[slot])

    def o_copy(k, slot):
        a, t = place(k)
        return pltpu.make_async_copy(obuf.at[slot], out_ref.at[a, t], osem.at[slot])

    g_copy(0, 0).start()
    held = (high.at[:count], low.at[:count])
    if not opening:
        row_copies = [pltpu.make_async_copy(rows_in[k], held[k], psem.at[k]) for k in range(2)]
        for copy in row_copies:
            copy.start()
    w0h[...], w0l[...] = split(w0_ref[...])
    w1h[...], w1l[...] = split(w1_ref[...])
    lh[...], ll[...] = split(l10_ref[...])

    mid = n // 2

    def times_lower(x, yh, yl):
        head = product((x[0][:, :mid], x[1][:, :mid]), (yh[:mid, :mid], yl[:mid, :mid]), 1)
        return jnp.concatenate([head, product(x, (yh[mid:, :], yl[mid:, :]), 1)], 1)

    def solve(k, carry):
        at = k if opening else k + count
        pltpu.make_async_copy(sets[0][0], raw.at[k, 0], rsem.at[k, 0]).wait()
        p0 = times_lower(split(raw[k, 0]), w0h, w0l)
        high[at, 0], low[at, 0] = split(p0)
        pltpu.make_async_copy(sets[0][0], raw.at[k, 1], rsem.at[k, 1]).wait()

        def strip(c, carry):
            part = pl.ds(pl.multiple_of(c * mid, mid), mid)
            whole = (high[at, 0], low[at, 0])
            raw[k, 1, :, part] = raw[k, 1, :, part] - product(whole, (lh[part, :], ll[part, :]), 1)
            return carry

        lax.fori_loop(0, 2, strip, 0)
        p1 = times_lower(split(raw[k, 1]), w1h, w1l)
        high[at, 1], low[at, 1] = split(p1)
        if opening:

            @pl.when(k < count)
            def _():
                keep[k, 0] = p0
                keep[k, 1] = p1

        return carry

    lax.fori_loop(0, total, solve, 0)
    if opening:
        row_copies = [pltpu.make_async_copy(held[k], rows_out[k], psem.at[k]) for k in range(2)]
        for copy in row_copies:
            copy.start()
    else:
        for copy in row_copies:
            copy.wait()

    last = count * len(steps)

    def update(k, carry):
        slot = lax.rem(k, 2)
        a, t = place(k)
        e = k // count
        g_copy(k, slot).wait()

        @pl.when(k + 1 < last)
        def _():
            g_copy(k + 1, 1 - slot).start()

        @pl.when(k >= 2)
        def _():
            o_copy(k - 2, slot).wait()

        first_tile = (t == 0) & (col < 2) if opening else jnp.bool_(False)
        is_row0 = (a == 0) & (row0 == 1)
        is_row1 = (a == 0) & (row1 == 1)
        special = is_row0 | is_row1
        plain = jnp.logical_not(first_tile)

        @pl.when(plain & jnp.logical_not(special))
        def _():
            def strip(c, carry):
                at = pl.ds(pl.multiple_of(c * mid, mid), mid)
                value = gbuf[slot, :, at]
                for panel in range(2):
                    column_part = (high[count + e, panel, at, :], low[count + e, panel, at, :])
                    value = value - product((high[a, panel], low[a, panel]), column_part, 1)
                obuf[slot, :, at] = value
                return carry

            lax.fori_loop(0, 2, strip, 0)

        @pl.when(plain & special)
        def _():
            obuf[slot] = jnp.zeros((n, n), jnp.float32)

        if opening:

            @pl.when(first_tile & jnp.logical_not(special))
            def _():
                obuf[slot] = keep[a, col]

            @pl.when(first_tile & is_row0)
            def _():
                obuf[slot] = jnp.where(col == 0, l0_ref[...], 0.0)

            @pl.when(first_tile & is_row1)
            def _():
                obuf[slot] = jnp.where(col == 0, l10_ref[...], l1_ref[...])

        o_copy(k, slot).start()
        return carry

    lax.fori_loop(0, last, update, 0)
    o_copy(last - 2, lax.rem(last, 2)).wait()
    o_copy(last - 1, lax.rem(last + 1, 2)).wait()
    if opening:
        for copy in row_copies:
            copy.wait()


def finish(grid, blocks, factors, steps, sets, own=None, before=None):
    count, width, n, _ = blocks.shape
    opening = before is None
    total = len(steps) + (count if opening else 0)
    scalars = jnp.stack(
        [
            grid.core,
            (grid.lo == grid.core).astype(jnp.int32),
            grid.hi // grid.ys,
            (grid.row == 0).astype(jnp.int32),
            (grid.row == 1).astype(jnp.int32),
            grid.col,
        ]
    ).astype(jnp.int32)
    inputs = [scalars, blocks, *factors]
    if opening:
        inputs += own
    for group in sets:
        inputs += group
    aliases = {}
    if not opening:
        aliases[len(inputs)] = 0
        inputs += before
    anywhere = pl.BlockSpec(memory_space=pl.ANY)
    vmem = pl.BlockSpec(memory_space=pltpu.VMEM)
    result = jax.ShapeDtypeStruct(blocks.shape, jnp.float32)
    panel = jax.ShapeDtypeStruct((count, 2, n, n), jnp.bfloat16)
    half = pltpu.VMEM((n, n), jnp.bfloat16)
    pair = pltpu.VMEM((2, n, n), jnp.float32)
    panels = pltpu.VMEM((count + len(steps), 2, n, n), jnp.bfloat16)
    return pl.pallas_call(
        functools.partial(finish_kernel, (count, width, n), steps, opening),
        out_shape=[result, panel, panel] if opening else [result],
        in_specs=[pl.BlockSpec(memory_space=pltpu.SMEM), anywhere] + [vmem] * 5 + [anywhere] * (len(inputs) - 7),
        out_specs=[anywhere] * (3 if opening else 1),
        scratch_shapes=[
            pltpu.VMEM((total, 2, n, n), jnp.float32),
            panels,
            panels,
            pltpu.VMEM((count, 2, n, n), jnp.float32),
            half,
            half,
            half,
            half,
            half,
            half,
            pair,
            pair,
            pltpu.SemaphoreType.DMA((total, 2)),
            pltpu.SemaphoreType.DMA((2,)),
            pltpu.SemaphoreType.DMA((2,)),
            pltpu.SemaphoreType.DMA((2,)),
        ],
        input_output_aliases=aliases,
        cost_estimate=pl.CostEstimate(flops=20_000_000_000, bytes_accessed=60_000_000, transcendentals=0),
        compiler_params=pltpu.CompilerParams(vmem_limit_bytes=58 * 1024 * 1024),
    )(*inputs)


def shards(gram_tiles):
    blocks = gram_tiles[:, 0, :, 0]
    grid = Grid()
    n = blocks.shape[-1]
    slots = range(blocks.shape[0])
    raw = [blocks[a, 0] for a in slots]

    def up():
        return [
            grid.send(blocks[:, 0], lambda hi, lo, y, core: (hi, lo, h, core) if y == 0 else None)
            for h in range(1, grid.ys)
        ]

    def own_tile(a, got):
        tile = raw[a]
        for h in range(1, grid.ys):
            tile = jnp.where(grid.y == h, got[h - 1][a], tile)
        return tile

    def pair_start(tile):
        return [grid.swap_hi(tile, s) for s in range(1, grid.ys)]

    def pair_finish(tile, got):
        same = tile
        for s in range(1, grid.ys):
            same = jnp.where((grid.hi % grid.ys) ^ grid.y == s, got[s - 1], same)
        return same

    def cross(tile):
        if grid.ys == 2:
            return grid.send(tile, lambda hi, lo, y, core: (3 - hi, lo, y, core) if hi in (1, 2) else None)
        return grid.swap_hi(tile, grid.ys)

    def spread(tile):
        return grid.swap_hi(tile, 1) if grid.ys == 2 else tile

    def far_tile(middle, edge):
        return jnp.where((grid.hi == 1) | (grid.hi == 2), middle, edge) if grid.ys == 2 else middle

    part, sides = scatter(grid, raw[0])
    lifted = up()
    corner = merge(grid, *gather(grid, part))
    sides = gather(grid, after(sides, part))
    own = [own_tile(a, lifted) for a in slots]
    paired = [pair_start(own[0]), None]
    paired[1] = pair_start(own[1])
    x = after(unpack_lower(n, corner), *own)

    a, l, w = factor_open(x)

    got = lax.optimization_barrier((paired[0], a))[0]
    near = [pair_finish(own[0], got), None]
    middle = [cross(near[0]), None]
    near_x = [grid.swap_lo(near[0]), None]
    a = after(a, near[0])
    l0, w0 = factor_close(a, l, w)

    got, mid, sides = lax.optimization_barrier((paired[1], middle[0], sides, w0))[:3]
    middle[0] = mid
    near[1] = pair_finish(own[1], got)
    edge = [spread(middle[0]), None]
    middle[1] = cross(near[1])
    near_x[1] = grid.swap_lo(near[1])
    side0, side1 = unpack_sides(n, merge(grid, *sides))
    side0 = after(side0, near[1])
    l10, a, l, w = factor_corner(side0, side1, w0)

    eg, mid, nx = lax.optimization_barrier((edge[0], middle[1], near_x[0], a))[:3]
    edge[0], middle[1], near_x[0] = eg, mid, nx
    far = [far_tile(middle[0], edge[0]), None]
    edge[1] = spread(middle[1])
    far_x = [grid.swap_lo(far[0]), None]
    own_got = [grid.swap_core(after(own[k], a)) for k in slots]
    near_got = [grid.swap_core(after(near[k], a)) for k in slots]
    near_x_got = [grid.swap_core(near_x[0]), None]
    a = after(a, far[0])
    l1, w1 = factor_close(a, l, w)

    eg, fx, nx = lax.optimization_barrier((edge[1], far_x[0], near_x[1], w1))[:3]
    edge[1], far_x[0], near_x[1] = eg, fx, nx
    far[1] = far_tile(middle[1], edge[1])
    far_x[1] = grid.swap_lo(far[1])
    far_got = [grid.swap_core(far[k]) for k in slots]
    near_x_got[1] = grid.swap_core(near_x[1])
    far_x_got = [grid.swap_core(far_x[0]), None]
    factors = (l0, l10, l1, w0, after(w1, far[1]))

    def groups(k, far_one):
        if far_one:
            return [far[k], far_got[k], far_x[k], far_x_got[k]]
        return [near[k], near_got[k], near_x[k], near_x_got[k]]

    steps = [(k, f) for k in slots for f in (0, 1)]
    head, rest = tuple(steps[:-1]), tuple(steps[-1:])
    done = finish(grid, blocks, factors, head, [groups(*step) for step in head], [*own, *own_got])
    far_x[1] = after(far_x[1], done[0])
    far_x_got[1] = grid.swap_core(far_x[1])
    blocks = finish(grid, blocks, factors, rest, [groups(*step) for step in rest], before=list(done))[0]
    return blocks[:, None, :, None]


def solution(mesh):
    devices = mesh.devices
    mesh = jax.sharding.Mesh(devices.reshape(devices.shape[0], -1, 2), AXES)
    placed = P(None, "row", None, ("y", "core"), None, None)
    return jax.shard_map(shards, mesh=mesh, in_specs=(placed,), out_specs=placed, check_vma=False)
```

profile of v0, /device:TPU:5, one launch (start us, length us, event | category | flops | bytes accessed | tf_op | source)
XLA Modules:
  0.0 266.8 jit_solution(8463158993212592352)
XLA Ops:
  0.0 1.3 slice_bitcast_fusion.4
  1.5 1.1 pad_maximum_fusion.5
  2.6 6.4 %all-to-all-start = ((f32[32,64,128]{2,1,0:T(8,128)}), f32[32,64,128]{2,1,0:T(8,128)S(1)}, u32[]{:S(2)}, u32[]{:S(2)}) async-start(f32[32,64,128]{2,1,0:T(8,128)} %pad_maximum_fusion.5), calls=%async_computation | async-start | bytes 2097152 | tf_op jit(solution)/shard_map/all_to_all | solution.py:229
  9.0 3.1 %slice_bitcast_fusion = f32[2,512,512]{2,1,0:T(8,128)} fusion(f32[2,4,512,512]{3,2,1,0:T(8,128)} %bitcast.192), kind=kLoop, calls=%fused_computation | loop fusion | bytes 4194304 | tf_op jit(solution)/shard_map/squeeze | solution.py:511
  12.1 1.3 collective-permute-start.1
  13.4 21.3 %all-to-all-done = f32[32,64,128]{2,1,0:T(8,128)S(1)} async-done(((f32[32,64,128]{2,1,0:T(8,128)}), f32[32,64,128]{2,1,0:T(8,128)S(1)}, u32[]{:S(2)}, u32[]{:S(2)}) %all-to-all-start) | async-done | bytes 1048608 | tf_op jit(solution)/shard_map/all_to_all | solution.py:229
  34.7 0.8 broadcast_in_dim.17
  35.5 4.7 %all-to-all-start.1 = ((f32[16,40,128]{2,1,0:T(8,128)}), f32[16,40,128]{2,1,0:T(8,128)S(1)}, u32[]{:S(2)}, u32[]{:S(2)}) async-start(f32[16,40,128]{2,1,0:T(8,128)} %broadcast_in_dim.17), calls=%async_computation.1 | async-start | bytes 655360 | tf_op jit(solution)/shard_map/all_to_all | solution.py:236
  40.2 31.1 %all-to-all-done.1 = f32[16,40,128]{2,1,0:T(8,128)S(1)} async-done(((f32[16,40,128]{2,1,0:T(8,128)}), f32[16,40,128]{2,1,0:T(8,128)S(1)}, u32[]{:S(2)}, u32[]{:S(2)}) %all-to-all-start.1) | async-done | bytes 327712 | tf_op jit(solution)/shard_map/all_to_all | solution.py:236
  71.3 1.0 broadcast_in_dim.18
  72.2 5.6 %all-to-all-start.2 = ((f32[16,104,128]{2,1,0:T(8,128)}), f32[16,104,128]{2,1,0:T(8,128)S(1)}, u32[]{:S(2)}, u32[]{:S(2)}) async-start(f32[16,104,128]{2,1,0:T(8,128)} %broadcast_in_dim.18), calls=%async_computation.2 | async-start | bytes 1703936 | tf_op jit(solution)/shard_map/all_to_all | solution.py:236
  77.9 1.0 collective-permute-start
  78.9 2.6 fusion.6
  81.5 1.2 collective-permute-start.2
  83.3 1.1 fusion.2.x_ref
  84.3 18.9 %shard_map.17 = (f32[256,256]{1,0:T(8,128)}, f32[512,512]{1,0:T(8,128)}, f32[512,512]{1,0:T(8,128)}) custom-call(f32[512,512]{1,0:T(8,128)} %fusion.2.x_ref), custom_call_target="tpu_custom_call" | custom-call | flops 20000000000 | bytes 60000000 | tf_op jit(solution)/shard_map/pallas_call | solution.py:133
  103.2 12.6 %collective-permute-done.2 = f32[512,512]{1,0:T(8,128)} collective-permute-done((f32[512,512]{1,0:T(8,128)S(1)}, f32[512,512]{1,0:T(8,128)}, u32[]{:S(2)}, u32[]{:S(2)}) %collective-permute-start.2) | collective-permute-done | bytes 1048608 | tf_op jit(solution)/shard_map/ppermute | solution.py:185
  115.8 2.4 broadcast_select_fusion.3.refs_10_
  118.2 1.6 collective-permute-start.4
  119.8 1.2 collective-permute-start.8
  121.0 2.7 %collective-permute-start.5 = (f32[16,104,128]{2,1,0:T(8,128)S(1)}, f32[16,104,128]{2,1,0:T(8,128)}, u32[]{:S(2)}, u32[]{:S(2)}) collective-permute-start(f32[16,104,128]{2,1,0:T(8,128)S(1)} %all-to-all-done.2), channel_id=1, source_target_pairs={{0,1},{1,0},{2,3},{3,2},{4,5},{5,4},{6,7},{7,6},{8,9},{9,8},{10,11... | collective-permute-start | bytes 2555912 | tf_op jit(solution)/shard_map/ppermute | solution.py:185
  123.7 18.2 %shard_map.18 = (f32[512,512]{1,0:T(8,128)}, f32[512,512]{1,0:T(8,128)}) custom-call(f32[256,256]{1,0:T(8,128)} %get-tuple-element.43.rest_ref, f32[512,512]{1,0:T(8,128)} %get-tuple-element.44.l_in, f32[512,512]{1,0:T(8,128)} %get-tuple-element.45.w_in), custom_call_target="tpu_custom_call" | custom-call | flops 20000000000 | bytes 60000000 | tf_op jit(solution)/shard_map/pallas_call | solution.py:133
  141.9 1.3 select_bitcast_fusion.1
  143.4 2.5 broadcast_select_fusion.2.refs_18_
  145.9 1.7 collective-permute-start.7
  148.0 1.1 maximum_maximum_fusion.side_ref
  149.1 4.3 %collective-permute-start.6 = (f32[512,512]{1,0:T(8,128)}, f32[512,512]{1,0:T(8,128)}, u32[]{:S(2)}, u32[]{:S(2)}) collective-permute-start(f32[512,512]{1,0:T(8,128)} %collective-permute-done.4), channel_id=1, source_target_pairs={{0,8},{1,9},{2,10},{3,11},{4,12},{5,13},{6,14},{7,15},{8,0},{9,1},... | collective-permute-start | bytes 3145736 | tf_op jit(solution)/shard_map/ppermute | solution.py:185
  153.3 1.1 fusion.5.x_ref
  154.4 24.1 %shard_map.19 = (f32[512,512]{1,0:T(8,128)}, f32[256,256]{1,0:T(8,128)}, f32[512,512]{1,0:T(8,128)}, f32[512,512]{1,0:T(8,128)}) custom-call(f32[512,512]{1,0:T(8,128)} %maximum_maximum_fusion.side_ref, f32[512,512]{1,0:T(8,128)} %fusion.5.x_ref, f32[512,512]{1,0:T(8,128)} %get-tuple-element.47.inverse_ref.refs_4_), custom_call_target="tpu_custom_call" | custom-call | flops 20000000000 | bytes 60000000 | tf_op jit(solution)/shard_map/pallas_call | solution.py:133
  178.5 4.2 %collective-permute-start.20 = (f32[512,512]{1,0:T(8,128)}, f32[512,512]{1,0:T(8,128)}, u32[]{:S(2)}, u32[]{:S(2)}) collective-permute-start(f32[512,512]{1,0:T(8,128)} %broadcast_select_fusion.2.refs_18_), channel_id=1, source_target_pairs={{0,1},{1,0},{2,3},{3,2},{4,5},{5,4},{6,7},{7,6},{8,9},{9,8},{10,11... | collective-permute-start | bytes 3145736 | tf_op jit(solution)/shard_map/ppermute | solution.py:185
  182.8 0.4 collective-permute-start.14
  183.2 1.4 broadcast_select_fusion.1.refs_14_
  185.0 18.2 %shard_map.20 = (f32[512,512]{1,0:T(8,128)}, f32[512,512]{1,0:T(8,128)}) custom-call(f32[256,256]{1,0:T(8,128)} %get-tuple-element.56.rest_ref, f32[512,512]{1,0:T(8,128)} %get-tuple-element.57.l_in, f32[512,512]{1,0:T(8,128)} %get-tuple-element.58.w_in), custom_call_target="tpu_custom_call" | custom-call | flops 20000000000 | bytes 60000000 | tf_op jit(solution)/shard_map/pallas_call | solution.py:133
  203.2 6.3 %collective-permute-done.10.refs_16_ = f32[512,512]{1,0:T(8,128)} collective-permute-done((f32[512,512]{1,0:T(8,128)S(1)}, f32[512,512]{1,0:T(8,128)}, u32[]{:S(2)}, u32[]{:S(2)}) %collective-permute-start.10) | collective-permute-done | bytes 1048608 | tf_op jit(solution)/shard_map/ppermute | solution.py:185
  209.5 0.9 collective-permute-start.15
  210.4 0.5 collective-permute-start.18
  211.0 0.4 collective-permute-start.19
  211.5 0.7 stack.118.scalars
  212.2 1.4 broadcast_select_fusion.refs_6_
  213.6 1.2 collective-permute-start.13
  214.9 0.7 collective-permute-start.12
  215.9 1.5 collective-permute-done.19.refs_17_
  217.4 1.4 collective-permute-done.21.refs_21_
  218.7 1.0 copy-done.4
  219.7 31.8 %shard_map.21 = (f32[2,4,512,512]{3,2,1,0:T(8,128)}, bf16[2,2,512,512]{3,2,1,0:T(8,128)(2,1)}, bf16[2,2,512,512]{3,2,1,0:T(8,128)(2,1)}) custom-call(s32[6]{0:T(128)} %stack.118.scalars, f32[2,4,512,512]{3,2,1,0:T(8,128)} %bitcast.194, f32[512,512]{1,0:T(8,128)} %get-tuple-element.46.refs_1_, f32[512,512]{1,0:T(8,128)} %get-tuple-element.52.refs_2_, ...), custom_call_target="tpu_custom_call" | custom-call | flops 20000000000 | bytes 60000000 | tf_op jit(solution)/shard_map/pallas_call | solution.py:473
  252.0 2.3 collective-permute-done.22.refs_9_
  254.3 1.0 copy-done.7
  255.2 11.4 %shard_map.22 = f32[2,4,512,512]{3,2,1,0:T(8,128)} custom-call(s32[6]{0:T(128)} %stack.118.scalars, f32[2,4,512,512]{3,2,1,0:T(8,128)} %bitcast.195, f32[512,512]{1,0:T(8,128)} %get-tuple-element.46.refs_1_, f32[512,512]{1,0:T(8,128)} %get-tuple-element.52.refs_2_, f32[512,512]{1,0:T(8,128)} %get-tuple-element.59.refs_3_, ...), custom_call_target="tpu_custom_call", output_to_operand_aliasing={{}: (11, {})} | custom-call | flops 20000000000 | bytes 60000000 | tf_op jit(solution)/shard_map/pallas_call | solution.py:473
  (64 shorter events, 2.6 us)
Async XLA Ops:
  2.6 32.1 %all-to-all-start = ((f32[32,64,128]{2,1,0:T(8,128)}), f32[32,64,128]{2,1,0:T(8,128)S(1)}, u32[]{:S(2)}, u32[]{:S(2)}) async-start(f32[32,64,128]{2,1,0:T(8,128)} %pad_maximum_fusion.5), calls=%async_computation | async-start | bytes 2097152 | tf_op jit(solution)/shard_map/all_to_all | solution.py:229
  12.1 66.8 %collective-permute-start.1 = (f32[2,512,512]{2,1,0:T(8,128)}, f32[2,512,512]{2,1,0:T(8,128)}, u32[]{:S(2)}, u32[]{:S(2)}) collective-permute-start(f32[2,512,512]{2,1,0:T(8,128)} %slice_bitcast_fusion), channel_id=1, source_target_pairs={{0,2},{1,3},{4,6},{5,7},{8,10},{9,11},{12,14},{13,15},{16,18},{17,... | collective-permute-start | bytes 6291464 | tf_op jit(solution)/shard_map/ppermute | solution.py:185
  35.5 35.8 %all-to-all-start.1 = ((f32[16,40,128]{2,1,0:T(8,128)}), f32[16,40,128]{2,1,0:T(8,128)S(1)}, u32[]{:S(2)}, u32[]{:S(2)}) async-start(f32[16,40,128]{2,1,0:T(8,128)} %broadcast_in_dim.17), calls=%async_computation.1 | async-start | bytes 655360 | tf_op jit(solution)/shard_map/all_to_all | solution.py:236
  72.2 48.7 %all-to-all-start.2 = ((f32[16,104,128]{2,1,0:T(8,128)}), f32[16,104,128]{2,1,0:T(8,128)S(1)}, u32[]{:S(2)}, u32[]{:S(2)}) async-start(f32[16,104,128]{2,1,0:T(8,128)} %broadcast_in_dim.18), calls=%async_computation.2 | async-start | bytes 1703936 | tf_op jit(solution)/shard_map/all_to_all | solution.py:236
  77.9 5.2 %collective-permute-start = (f32[16,40,128]{2,1,0:T(8,128)S(1)}, f32[16,40,128]{2,1,0:T(8,128)S(1)}, u32[]{:S(2)}, u32[]{:S(2)}) collective-permute-start(f32[16,40,128]{2,1,0:T(8,128)S(1)} %all-to-all-done.1), channel_id=1, source_target_pairs={{0,1},{1,0},{2,3},{3,2},{4,5},{5,4},{6,7},{7,6},{8,9},{9,8},{10,11... | collective-permute-start | bytes 983048 | tf_op jit(solution)/shard_map/ppermute | solution.py:185
  81.5 101.3 %copy-start.1 = (f32[512,512]{1,0:T(8,128)}, f32[512,512]{1,0:T(8,128)S(1)}, u32[]{:S(2)}) copy-start(f32[512,512]{1,0:T(8,128)S(1)} %get-tuple-element.64.refs_6_) | copy-start | bytes 3145732
  81.5 128.0 %copy-start = (f32[512,512]{1,0:T(8,128)}, f32[512,512]{1,0:T(8,128)S(1)}, u32[]{:S(2)}) copy-start(f32[512,512]{1,0:T(8,128)S(1)} %get-tuple-element.65.refs_7_) | copy-start | bytes 3145732
  81.5 34.2 %collective-permute-start.2 = (f32[512,512]{1,0:T(8,128)S(1)}, f32[512,512]{1,0:T(8,128)}, u32[]{:S(2)}, u32[]{:S(2)}) collective-permute-start(f32[512,512]{1,0:T(8,128)S(1)} %get-tuple-element.64.refs_6_), channel_id=1, source_target_pairs={{0,8},{1,9},{2,10},{3,11},{4,12},{5,13},{6,14},{7,15},{8,0},{9,1},... | collective-permute-start | bytes 3145736 | tf_op jit(solution)/shard_map/ppermute | solution.py:185
  82.8 59.1 %collective-permute-start.3 = (f32[512,512]{1,0:T(8,128)S(1)}, f32[512,512]{1,0:T(8,128)}, u32[]{:S(2)}, u32[]{:S(2)}) collective-permute-start(f32[512,512]{1,0:T(8,128)S(1)} %get-tuple-element.65.refs_7_), channel_id=1, source_target_pairs={{0,8},{1,9},{2,10},{3,11},{4,12},{5,13},{6,14},{7,15},{8,0},{9,1},... | collective-permute-start | bytes 3145736 | tf_op jit(solution)/shard_map/ppermute | solution.py:185
  118.2 23.8 %collective-permute-start.4 = (f32[512,512]{1,0:T(8,128)}, f32[512,512]{1,0:T(8,128)}, u32[]{:S(2)}, u32[]{:S(2)}) collective-permute-start(f32[512,512]{1,0:T(8,128)} %broadcast_select_fusion.3.refs_10_), channel_id=1, source_target_pairs={{8,16},{9,17},{10,18},{11,19},{12,20},{13,21},{14,22},{15,23},{16,... | collective-permute-start | bytes 3145736 | tf_op jit(solution)/shard_map/ppermute | solution.py:185
  119.8 62.9 %collective-permute-start.8 = (f32[512,512]{1,0:T(8,128)}, f32[512,512]{1,0:T(8,128)}, u32[]{:S(2)}, u32[]{:S(2)}) collective-permute-start(f32[512,512]{1,0:T(8,128)} %broadcast_select_fusion.3.refs_10_), channel_id=1, source_target_pairs={{0,4},{1,5},{2,6},{3,7},{4,0},{5,1},{6,2},{7,3},{8,12},{9,13},{10,... | collective-permute-start | bytes 3145736 | tf_op jit(solution)/shard_map/ppermute | solution.py:185
  121.0 20.9 %collective-permute-start.5 = (f32[16,104,128]{2,1,0:T(8,128)S(1)}, f32[16,104,128]{2,1,0:T(8,128)}, u32[]{:S(2)}, u32[]{:S(2)}) collective-permute-start(f32[16,104,128]{2,1,0:T(8,128)S(1)} %all-to-all-done.2), channel_id=1, source_target_pairs={{0,1},{1,0},{2,3},{3,2},{4,5},{5,4},{6,7},{7,6},{8,9},{9,8},{10,11... | collective-permute-start | bytes 2555912 | tf_op jit(solution)/shard_map/ppermute | solution.py:185
  145.9 36.9 %collective-permute-start.7 = (f32[512,512]{1,0:T(8,128)}, f32[512,512]{1,0:T(8,128)}, u32[]{:S(2)}, u32[]{:S(2)}) collective-permute-start(f32[512,512]{1,0:T(8,128)} %broadcast_select_fusion.2.refs_18_), channel_id=1, source_target_pairs={{8,16},{9,17},{10,18},{11,19},{12,20},{13,21},{14,22},{15,23},{16,... | collective-permute-start | bytes 3145736 | tf_op jit(solution)/shard_map/ppermute | solution.py:185
  147.6 37.5 %collective-permute-start.11 = (f32[512,512]{1,0:T(8,128)}, f32[512,512]{1,0:T(8,128)}, u32[]{:S(2)}, u32[]{:S(2)}) collective-permute-start(f32[512,512]{1,0:T(8,128)} %broadcast_select_fusion.2.refs_18_), channel_id=1, source_target_pairs={{0,4},{1,5},{2,6},{3,7},{4,0},{5,1},{6,2},{7,3},{8,12},{9,13},{10,... | collective-permute-start | bytes 3145736 | tf_op jit(solution)/shard_map/ppermute | solution.py:185
  149.1 34.2 %collective-permute-start.6 = (f32[512,512]{1,0:T(8,128)}, f32[512,512]{1,0:T(8,128)}, u32[]{:S(2)}, u32[]{:S(2)}) collective-permute-start(f32[512,512]{1,0:T(8,128)} %collective-permute-done.4), channel_id=1, source_target_pairs={{0,8},{1,9},{2,10},{3,11},{4,12},{5,13},{6,14},{7,15},{8,0},{9,1},... | collective-permute-start | bytes 3145736 | tf_op jit(solution)/shard_map/ppermute | solution.py:185
  178.5 32.4 %collective-permute-start.20 = (f32[512,512]{1,0:T(8,128)}, f32[512,512]{1,0:T(8,128)}, u32[]{:S(2)}, u32[]{:S(2)}) collective-permute-start(f32[512,512]{1,0:T(8,128)} %broadcast_select_fusion.2.refs_18_), channel_id=1, source_target_pairs={{0,1},{1,0},{2,3},{3,2},{4,5},{5,4},{6,7},{7,6},{8,9},{9,8},{10,11... | collective-permute-start | bytes 3145736 | tf_op jit(solution)/shard_map/ppermute | solution.py:185
  182.7 28.3 %collective-permute-start.16 = (f32[512,512]{1,0:T(8,128)}, f32[512,512]{1,0:T(8,128)}, u32[]{:S(2)}, u32[]{:S(2)}) collective-permute-start(f32[512,512]{1,0:T(8,128)} %broadcast_select_fusion.3.refs_10_), channel_id=1, source_target_pairs={{0,1},{1,0},{2,3},{3,2},{4,5},{5,4},{6,7},{7,6},{8,9},{9,8},{10,11... | collective-permute-start | bytes 3145736 | tf_op jit(solution)/shard_map/ppermute | solution.py:185
  182.8 28.7 %collective-permute-start.14 = (f32[512,512]{1,0:T(8,128)S(1)}, f32[512,512]{1,0:T(8,128)}, u32[]{:S(2)}, u32[]{:S(2)}) collective-permute-start(f32[512,512]{1,0:T(8,128)S(1)} %get-tuple-element.64.refs_6_), channel_id=1, source_target_pairs={{0,1},{1,0},{2,3},{3,2},{4,5},{5,4},{6,7},{7,6},{8,9},{9,8},{10,11... | collective-permute-start | bytes 3145736 | tf_op jit(solution)/shard_map/ppermute | solution.py:185
  184.7 25.8 %copy-start.2 = (f32[512,512]{1,0:T(8,128)}, f32[512,512]{1,0:T(8,128)S(1)}, u32[]{:S(2)}) copy-start(f32[512,512]{1,0:T(8,128)S(1)} %broadcast_select_fusion.1.refs_14_) | copy-start | bytes 3145732
  184.7 24.8 %collective-permute-start.10 = (f32[512,512]{1,0:T(8,128)S(1)}, f32[512,512]{1,0:T(8,128)}, u32[]{:S(2)}, u32[]{:S(2)}) collective-permute-start(f32[512,512]{1,0:T(8,128)S(1)} %broadcast_select_fusion.1.refs_14_), channel_id=1, source_target_pairs={{0,4},{1,5},{2,6},{3,7},{4,0},{5,1},{6,2},{7,3},{8,12},{9,13},{10,... | collective-permute-start | bytes 3145736 | tf_op jit(solution)/shard_map/ppermute | solution.py:185
  185.0 25.4 %collective-permute-start.9 = (f32[512,512]{1,0:T(8,128)}, f32[512,512]{1,0:T(8,128)}, u32[]{:S(2)}, u32[]{:S(2)}) collective-permute-start(f32[512,512]{1,0:T(8,128)} %collective-permute-done.7), channel_id=1, source_target_pairs={{0,8},{1,9},{2,10},{3,11},{4,12},{5,13},{6,14},{7,15},{8,0},{9,1},... | collective-permute-start | bytes 3145736 | tf_op jit(solution)/shard_map/ppermute | solution.py:185
  209.5 4.1 %collective-permute-start.15 = (f32[512,512]{1,0:T(8,128)S(1)}, f32[512,512]{1,0:T(8,128)}, u32[]{:S(2)}, u32[]{:S(2)}) collective-permute-start(f32[512,512]{1,0:T(8,128)S(1)} %get-tuple-element.65.refs_7_), channel_id=1, source_target_pairs={{0,1},{1,0},{2,3},{3,2},{4,5},{5,4},{6,7},{7,6},{8,9},{9,8},{10,11... | collective-permute-start | bytes 3145736 | tf_op jit(solution)/shard_map/ppermute | solution.py:185
  210.4 4.4 %collective-permute-start.18 = (f32[512,512]{1,0:T(8,128)S(1)}, f32[512,512]{1,0:T(8,128)}, u32[]{:S(2)}, u32[]{:S(2)}) collective-permute-start(f32[512,512]{1,0:T(8,128)S(1)} %broadcast_select_fusion.1.refs_14_), channel_id=1, source_target_pairs={{0,1},{1,0},{2,3},{3,2},{4,5},{5,4},{6,7},{7,6},{8,9},{9,8},{10,11... | collective-permute-start | bytes 3145736 | tf_op jit(solution)/shard_map/ppermute | solution.py:185
  210.9 4.9 %collective-permute-start.17 = (f32[512,512]{1,0:T(8,128)}, f32[512,512]{1,0:T(8,128)}, u32[]{:S(2)}, u32[]{:S(2)}) collective-permute-start(f32[512,512]{1,0:T(8,128)} %collective-permute-done.8.refs_12_), channel_id=1, source_target_pairs={{0,1},{1,0},{2,3},{3,2},{4,5},{5,4},{6,7},{7,6},{8,9},{9,8},{10,11... | collective-permute-start | bytes 3145736 | tf_op jit(solution)/shard_map/ppermute | solution.py:185
  211.0 6.3 %collective-permute-start.19 = (f32[512,512]{1,0:T(8,128)}, f32[512,512]{1,0:T(8,128)}, u32[]{:S(2)}, u32[]{:S(2)}) collective-permute-start(f32[512,512]{1,0:T(8,128)} %collective-permute-done.10.refs_16_), channel_id=1, source_target_pairs={{0,1},{1,0},{2,3},{3,2},{4,5},{5,4},{6,7},{7,6},{8,9},{9,8},{10,11... | collective-permute-start | bytes 3145736 | tf_op jit(solution)/shard_map/ppermute | solution.py:185
  211.5 7.3 %collective-permute-start.21 = (f32[512,512]{1,0:T(8,128)}, f32[512,512]{1,0:T(8,128)S(1)}, u32[]{:S(2)}, u32[]{:S(2)}) collective-permute-start(f32[512,512]{1,0:T(8,128)} %collective-permute-done.11.refs_20_), channel_id=1, source_target_pairs={{0,1},{1,0},{2,3},{3,2},{4,5},{5,4},{6,7},{7,6},{8,9},{9,8},{10,11... | collective-permute-start | bytes 3145736 | tf_op jit(solution)/shard_map/ppermute | solution.py:185
  213.6 37.9 %copy-start.3 = (f32[512,512]{1,0:T(8,128)}, f32[512,512]{1,0:T(8,128)S(1)}, u32[]{:S(2)}) copy-start(f32[512,512]{1,0:T(8,128)S(1)} %broadcast_select_fusion.refs_6_) | copy-start | bytes 3145732
  213.6 37.9 %collective-permute-start.13 = (f32[512,512]{1,0:T(8,128)S(1)}, f32[512,512]{1,0:T(8,128)S(1)}, u32[]{:S(2)}, u32[]{:S(2)}) collective-permute-start(f32[512,512]{1,0:T(8,128)S(1)} %broadcast_select_fusion.refs_6_), channel_id=1, source_target_pairs={{0,4},{1,5},{2,6},{3,7},{4,0},{5,1},{6,2},{7,3},{8,12},{9,13},{10,... | collective-permute-start | bytes 3145736 | tf_op jit(solution)/shard_map/ppermute | solution.py:185
  214.9 37.1 %collective-permute-start.12 = (f32[512,512]{1,0:T(8,128)S(1)}, f32[512,512]{1,0:T(8,128)S(1)}, u32[]{:S(2)}, u32[]{:S(2)}) collective-permute-start(f32[512,512]{1,0:T(8,128)S(1)} %broadcast_select_fusion.refs_6_), channel_id=1, source_target_pairs={{0,1},{1,0},{2,3},{3,2},{4,5},{5,4},{6,7},{7,6},{8,9},{9,8},{10,11... | collective-permute-start | bytes 3145736 | tf_op jit(solution)/shard_map/ppermute | solution.py:185
  218.7 1.0 copy-start.4
  251.5 2.7 %copy-start.5 = (f32[512,512]{1,0:T(8,128)}, f32[512,512]{1,0:T(8,128)S(1)}, u32[]{:S(2)}) copy-start(f32[512,512]{1,0:T(8,128)S(1)} %collective-permute-done.13.refs_8_) | copy-start | bytes 3145732
  251.5 2.7 %collective-permute-start.22 = (f32[512,512]{1,0:T(8,128)S(1)}, f32[512,512]{1,0:T(8,128)S(1)}, u32[]{:S(2)}, u32[]{:S(2)}) collective-permute-start(f32[512,512]{1,0:T(8,128)S(1)} %collective-permute-done.13.refs_8_), channel_id=1, source_target_pairs={{0,1},{1,0},{2,3},{3,2},{4,5},{5,4},{6,7},{7,6},{8,9},{9,8},{10,11... | collective-permute-start | bytes 3145736 | tf_op jit(solution)/shard_map/ppermute | solution.py:185
  252.0 2.3 copy-start.6
  254.2 1.0 copy-start.7
where the time goes:
time: 268 us; the launch traced here: 267 us
  Pallas kernels  123 us (46%)
  waiting for transfers between devices  76.7 us (29%)
  starting transfers between devices  41.7 us (16%)
  other arithmetic  16.2 us (6%)
  local copies, waits for them, and re-layouts  9.18 us (3%)
    pallas_call x4, Pallas kernels, call(): pl.pallas_call(kernel, out_shape=[jax.ShapeDtypeStruct((size, size), jnp....  79.4 us
    pallas_call x2, Pallas kernels, finish(): pl.pallas_call(functools.partial(finish_kernel, (count, width, n), steps,...  43.2 us
    all_to_all x2, waiting for transfers between devices, gather(): mine = lax.all_to_all(spread, ('row', 'y'), 0, 0, tiled=True)  31.1 us
    ppermute x23, starting transfers between devices, send(): return lax.ppermute(x, AXES, pairs)  25 us
    ppermute x23, waiting for transfers between devices, send(): return lax.ppermute(x, AXES, pairs)  24.3 us
    all_to_all x1, waiting for transfers between devices, scatter(): got = lax.all_to_all(jnp.concatenate(parts, 1), AXES, 0, 0, tiled=True)  21.3 us
    all_to_all x2, starting transfers between devices, gather(): mine = lax.all_to_all(spread, ('row', 'y'), 0, 0, tiled=True)  10.3 us
    all_to_all x1, starting transfers between devices, scatter(): got = lax.all_to_all(jnp.concatenate(parts, 1), AXES, 0, 0, tiled=True)  6.38 us
  transfers between devices with their start and end apart: 26, of which 8 were waited for; matrix products, arithmetic and copies ran while one was open for 8% of the time, Pallas kernels for 42%

commit v1 on v0

--- a/solution.py
+++ b/solution.py
@@ -506,16 +506,13 @@
     slots = range(blocks.shape[0])
     raw = [blocks[a, 0] for a in slots]
 
-    def up():
-        return [
-            grid.send(blocks[:, 0], lambda hi, lo, y, core: (hi, lo, h, core) if y == 0 else None)
-            for h in range(1, grid.ys)
-        ]
+    def up(a):
+        return [grid.send(raw[a], lambda hi, lo, y, core: (hi, lo, h, core) if y == 0 else None) for h in range(1, grid.ys)]
 
     def own_tile(a, got):
         tile = raw[a]
         for h in range(1, grid.ys):
-            tile = jnp.where(grid.y == h, got[h - 1][a], tile)
+            tile = jnp.where(grid.y == h, got[h - 1], tile)
         return tile
 
     def pair_start(tile):
@@ -539,21 +536,22 @@
         return jnp.where((grid.hi == 1) | (grid.hi == 2), middle, edge) if grid.ys == 2 else middle
 
     part, sides = scatter(grid, raw[0])
-    lifted = up()
+    lifted = [up(a) for a in slots]
     corner = merge(grid, *gather(grid, part))
     sides = gather(grid, after(sides, part))
-    own = [own_tile(a, lifted) for a in slots]
+    own = [own_tile(0, lifted[0]), None]
     paired = [pair_start(own[0]), None]
+    x = after(unpack_lower(n, corner), own[0])
+
+    a, l, w = factor_open(x)
+
+    got, lift = lax.optimization_barrier((paired[0], lifted[1], a))[:2]
+    near = [pair_finish(own[0], got), None]
+    own[1] = own_tile(1, lift)
+    middle = [cross(near[0]), None]
     paired[1] = pair_start(own[1])
-    x = after(unpack_lower(n, corner), *own)
-
-    a, l, w = factor_open(x)
-
-    got = lax.optimization_barrier((paired[0], a))[0]
-    near = [pair_finish(own[0], got), None]
-    middle = [cross(near[0]), None]
     near_x = [grid.swap_lo(near[0]), None]
-    a = after(a, near[0])
+    a = after(a, near[0], own[1])
     l0, w0 = factor_close(a, l, w)
 
     got, mid, sides = lax.optimization_barrier((paired[1], middle[0], sides, w0))[:3]

time: 268 us -> 234 us (0.87)
  waiting for transfers between devices: 76.7 us -> 43.7 us
    all_to_all x2, waiting for transfers between devices: 31.1 us -> 0.85 us  [gather(): mine = lax.all_to_all(spread, ('row', 'y'), 0, 0, tiled=True)]
    ppermute x23 -> x24, waiting for transfers between devices: 24.3 us -> 18.4 us  [send(): return lax.ppermute(x, AXES, pairs)]
    squeeze x1 -> x0, local copies, waits for them, and re-layouts: 3.09 us -> none  [up(): blocks[:, 0]]
    all_to_all x1, waiting for transfers between devices: 21.3 us -> 24.4 us  [scatter(): got = lax.all_to_all(jnp.concatenate(parts, 1), AXES, 0, 0, tiled=True)]
    ppermute x23 -> x24, starting transfers between devices: 25 us -> 24.8 us  [send(): return lax.ppermute(x, AXES, pairs)]
  transfers between devices with their start and end apart: 26 -> 27, of which waited for: 8 -> 9; matrix products, arithmetic and copies ran while one was open for 8% -> 8% of each run, Pallas kernels for 42% -> 48%
where the time goes in v1:
time: 234 us; the launch traced here: 233 us
  Pallas kernels  123 us (53%)
  waiting for transfers between devices  43.7 us (19%)
  starting transfers between devices  40.5 us (17%)
  other arithmetic  17.8 us (8%)
  local copies, waits for them, and re-layouts  7.47 us (3%)
    pallas_call x4, Pallas kernels, call(): pl.pallas_call(kernel, out_shape=[jax.ShapeDtypeStruct((size, size), jnp....  79.4 us
    pallas_call x2, Pallas kernels, finish(): pl.pallas_call(functools.partial(finish_kernel, (count, width, n), steps,...  43.2 us
    ppermute x24, starting transfers between devices, send(): return lax.ppermute(x, AXES, pairs)  24.8 us
    all_to_all x1, waiting for transfers between devices, scatter(): got = lax.all_to_all(jnp.concatenate(parts, 1), AXES, 0, 0, tiled=True)  24.4 us
    ppermute x24, waiting for transfers between devices, send(): return lax.ppermute(x, AXES, pairs)  18.4 us
    all_to_all x2, starting transfers between devices, gather(): mine = lax.all_to_all(spread, ('row', 'y'), 0, 0, tiled=True)  9.28 us
    all_to_all x1, starting transfers between devices, scatter(): got = lax.all_to_all(jnp.concatenate(parts, 1), AXES, 0, 0, tiled=True)  6.38 us
    select_n x2, other arithmetic, pair_finish(): same = jnp.where(grid.hi % grid.ys ^ grid.y == s, got[s - 1], same)  4.97 us
  transfers between devices with their start and end apart: 27, of which 9 were waited for; matrix products, arithmetic and copies ran while one was open for 8% of the time, Pallas kernels for 48%

profile of v1, /device:TPU:5, one launch (start us, length us, event | category | flops | bytes accessed | tf_op | source)
XLA Modules:
  0.0 232.5 jit_solution(16448467599567001457)
XLA Ops:
  0.0 2.7 %slice_bitcast_fusion = (f32[512,512]{1,0:T(8,128)}, f32[512,512]{1,0:T(8,128)S(1)}) fusion(f32[2,4,512,512]{3,2,1,0:T(8,128)} %bitcast.184), kind=kLoop, calls=%fused_computation.11 | loop fusion | bytes 4194304 | tf_op jit(solution)/shard_map/squeeze | solution.py:507
  2.9 1.1 pad_maximum_fusion.5
  4.0 6.4 %all-to-all-start = ((f32[32,64,128]{2,1,0:T(8,128)}), f32[32,64,128]{2,1,0:T(8,128)S(1)}, u32[]{:S(2)}, u32[]{:S(2)}) async-start(f32[32,64,128]{2,1,0:T(8,128)} %pad_maximum_fusion.5), calls=%async_computation | async-start | bytes 2097152 | tf_op jit(solution)/shard_map/all_to_all | solution.py:229
  10.4 1.3 collective-permute-start.1
  11.7 24.4 %all-to-all-done = f32[32,64,128]{2,1,0:T(8,128)S(1)} async-done(((f32[32,64,128]{2,1,0:T(8,128)}), f32[32,64,128]{2,1,0:T(8,128)S(1)}, u32[]{:S(2)}, u32[]{:S(2)}) %all-to-all-start) | async-done | bytes 1048608 | tf_op jit(solution)/shard_map/all_to_all | solution.py:229
  36.1 0.8 broadcast_in_dim.17
  36.9 4.7 %all-to-all-start.1 = ((f32[16,40,128]{2,1,0:T(8,128)}), f32[16,40,128]{2,1,0:T(8,128)S(1)}, u32[]{:S(2)}, u32[]{:S(2)}) async-start(f32[16,40,128]{2,1,0:T(8,128)} %broadcast_in_dim.17), calls=%async_computation.1 | async-start | bytes 655360 | tf_op jit(solution)/shard_map/all_to_all | solution.py:236
  41.6 1.3 collective-permute-start.3
  42.9 5.5 %collective-permute-done.1 = f32[512,512]{1,0:T(8,128)S(1)} collective-permute-done((f32[512,512]{1,0:T(8,128)S(1)}, f32[512,512]{1,0:T(8,128)S(1)}, u32[]{:S(2)}, u32[]{:S(2)}) %collective-permute-start.1) | collective-permute-done | bytes 1048608 | tf_op jit(solution)/shard_map/ppermute | solution.py:185
  48.4 1.4 broadcast_select_fusion.5.refs_6_
  49.9 0.8 all-to-all-done.1
  50.8 2.1 collective-permute-start
  52.9 1.0 broadcast_in_dim.18
  53.9 4.6 %all-to-all-start.2 = ((f32[16,104,128]{2,1,0:T(8,128)}), f32[16,104,128]{2,1,0:T(8,128)S(1)}, u32[]{:S(2)}, u32[]{:S(2)}) async-start(f32[16,104,128]{2,1,0:T(8,128)} %broadcast_in_dim.18), calls=%async_computation.2 | async-start | bytes 1703936 | tf_op jit(solution)/shard_map/all_to_all | solution.py:236
  58.5 1.0 select_bitcast_fusion.3
  59.6 1.1 fusion.2.x_ref
  60.7 18.8 %shard_map.17 = (f32[256,256]{1,0:T(8,128)}, f32[512,512]{1,0:T(8,128)}, f32[512,512]{1,0:T(8,128)}) custom-call(f32[512,512]{1,0:T(8,128)} %fusion.2.x_ref), custom_call_target="tpu_custom_call" | custom-call | flops 20000000000 | bytes 60000000 | tf_op jit(solution)/shard_map/pallas_call | solution.py:133
  79.5 1.2 collective-permute-done.2
  80.7 2.5 %broadcast_select_fusion.3.refs_10_ = f32[512,512]{1,0:T(8,128)} fusion(f32[512,512]{1,0:T(8,128)} %collective-permute-done.2, f32[512,512]{1,0:T(8,128)S(1)} %broadcast_select_fusion.5.refs_6_, pred[]{:T(512)S(6)} %eq.41), kind=kLoop, calls=%fused_computation.22 | loop fusion | flops 262144 | bytes 3145729 | tf_op jit(solution)/shard_map/jit(_where)/select_n | solution.py:524
  83.2 1.6 collective-permute-start.5
  84.9 1.7 broadcast_select_fusion.4.refs_7_
  86.6 1.8 collective-permute-start.4
  88.4 1.2 collective-permute-start.9
  89.6 2.6 %collective-permute-start.6 = (f32[16,104,128]{2,1,0:T(8,128)S(1)}, f32[16,104,128]{2,1,0:T(8,128)}, u32[]{:S(2)}, u32[]{:S(2)}) collective-permute-start(f32[16,104,128]{2,1,0:T(8,128)S(1)} %all-to-all-done.2), channel_id=1, source_target_pairs={{0,1},{1,0},{2,3},{3,2},{4,5},{5,4},{6,7},{7,6},{8,9},{9,8},{10,11... | collective-permute-start | bytes 2555912 | tf_op jit(solution)/shard_map/ppermute | solution.py:185
  92.2 18.2 %shard_map.18 = (f32[512,512]{1,0:T(8,128)}, f32[512,512]{1,0:T(8,128)}) custom-call(f32[256,256]{1,0:T(8,128)} %get-tuple-element.45.rest_ref, f32[512,512]{1,0:T(8,128)} %get-tuple-element.46.l_in, f32[512,512]{1,0:T(8,128)} %get-tuple-element.47.w_in), custom_call_target="tpu_custom_call" | custom-call | flops 20000000000 | bytes 60000000 | tf_op jit(solution)/shard_map/pallas_call | solution.py:133
  110.4 1.3 select_bitcast_fusion.1
  112.0 2.5 %broadcast_select_fusion.2.refs_18_ = f32[512,512]{1,0:T(8,128)} fusion(f32[512,512]{1,0:T(8,128)} %collective-permute-done.4, f32[512,512]{1,0:T(8,128)S(1)} %broadcast_select_fusion.4.refs_7_, pred[]{:T(512)S(6)} %eq.41), kind=kLoop, calls=%fused_computation.21 | loop fusion | flops 262144 | bytes 3145729 | tf_op jit(solution)/shard_map/jit(_where)/select_n | solution.py:524
  114.4 1.7 collective-permute-start.8
  116.1 1.3 collective-permute-start.12
  117.6 1.0 maximum_maximum_fusion.side_ref
  118.6 1.1 collective-permute-start.7
  119.8 1.1 fusion.5.x_ref
  120.8 24.1 %shard_map.19 = (f32[512,512]{1,0:T(8,128)}, f32[256,256]{1,0:T(8,128)}, f32[512,512]{1,0:T(8,128)}, f32[512,512]{1,0:T(8,128)}) custom-call(f32[512,512]{1,0:T(8,128)} %maximum_maximum_fusion.side_ref, f32[512,512]{1,0:T(8,128)} %fusion.5.x_ref, f32[512,512]{1,0:T(8,128)} %get-tuple-element.49.inverse_ref.refs_4_), custom_call_target="tpu_custom_call" | custom-call | flops 20000000000 | bytes 60000000 | tf_op jit(solution)/shard_map/pallas_call | solution.py:133
  144.9 3.5 %collective-permute-start.21 = (f32[512,512]{1,0:T(8,128)}, f32[512,512]{1,0:T(8,128)}, u32[]{:S(2)}, u32[]{:S(2)}) collective-permute-start(f32[512,512]{1,0:T(8,128)} %broadcast_select_fusion.2.refs_18_), channel_id=1, source_target_pairs={{0,1},{1,0},{2,3},{3,2},{4,5},{5,4},{6,7},{7,6},{8,9},{9,8},{10,11... | collective-permute-start | bytes 3145736 | tf_op jit(solution)/shard_map/ppermute | solution.py:185
  149.0 1.4 broadcast_select_fusion.1.refs_14_
  150.8 18.2 %shard_map.20 = (f32[512,512]{1,0:T(8,128)}, f32[512,512]{1,0:T(8,128)}) custom-call(f32[256,256]{1,0:T(8,128)} %get-tuple-element.58.rest_ref, f32[512,512]{1,0:T(8,128)} %get-tuple-element.59.l_in, f32[512,512]{1,0:T(8,128)} %get-tuple-element.60.w_in), custom_call_target="tpu_custom_call" | custom-call | flops 20000000000 | bytes 60000000 | tf_op jit(solution)/shard_map/pallas_call | solution.py:133
  168.9 6.3 %collective-permute-done.11.refs_16_ = f32[512,512]{1,0:T(8,128)} collective-permute-done((f32[512,512]{1,0:T(8,128)S(1)}, f32[512,512]{1,0:T(8,128)}, u32[]{:S(2)}, u32[]{:S(2)}) %collective-permute-start.11) | collective-permute-done | bytes 1048608 | tf_op jit(solution)/shard_map/ppermute | solution.py:185
  175.2 0.9 collective-permute-start.15
  177.9 1.4 broadcast_select_fusion.refs_6_
  179.4 1.3 collective-permute-start.14
  180.6 0.7 collective-permute-start.13
  181.6 1.5 collective-permute-done.20.refs_17_
  183.1 1.4 collective-permute-done.22.refs_21_
  184.5 1.0 copy-done.4
  185.4 31.8 %shard_map.21 = (f32[2,4,512,512]{3,2,1,0:T(8,128)}, bf16[2,2,512,512]{3,2,1,0:T(8,128)(2,1)}, bf16[2,2,512,512]{3,2,1,0:T(8,128)(2,1)}) custom-call(s32[6]{0:T(128)} %stack.118.scalars, f32[2,4,512,512]{3,2,1,0:T(8,128)} %bitcast.187, f32[512,512]{1,0:T(8,128)} %get-tuple-element.48.refs_1_, f32[512,512]{1,0:T(8,128)} %get-tuple-element.54.refs_2_, ...), custom_call_target="tpu_custom_call" | custom-call | flops 20000000000 | bytes 60000000 | tf_op jit(solution)/shard_map/pallas_call | solution.py:473
  217.7 2.3 collective-permute-done.23.refs_9_
  220.0 0.9 copy-done.7
  220.9 11.4 %shard_map.22 = f32[2,4,512,512]{3,2,1,0:T(8,128)} custom-call(s32[6]{0:T(128)} %stack.118.scalars, f32[2,4,512,512]{3,2,1,0:T(8,128)} %bitcast.188, f32[512,512]{1,0:T(8,128)} %get-tuple-element.48.refs_1_, f32[512,512]{1,0:T(8,128)} %get-tuple-element.54.refs_2_, f32[512,512]{1,0:T(8,128)} %get-tuple-element.61.refs_3_, ...), custom_call_target="tpu_custom_call", output_to_operand_aliasing={{}: (11, {})} | custom-call | flops 20000000000 | bytes 60000000 | tf_op jit(solution)/shard_map/pallas_call | solution.py:473
  (66 shorter events, 4.0 us)
Async XLA Ops:
  4.0 32.1 %all-to-all-start = ((f32[32,64,128]{2,1,0:T(8,128)}), f32[32,64,128]{2,1,0:T(8,128)S(1)}, u32[]{:S(2)}, u32[]{:S(2)}) async-start(f32[32,64,128]{2,1,0:T(8,128)} %pad_maximum_fusion.5), calls=%async_computation | async-start | bytes 2097152 | tf_op jit(solution)/shard_map/all_to_all | solution.py:229
  10.4 38.0 %collective-permute-start.1 = (f32[512,512]{1,0:T(8,128)S(1)}, f32[512,512]{1,0:T(8,128)S(1)}, u32[]{:S(2)}, u32[]{:S(2)}) collective-permute-start(f32[512,512]{1,0:T(8,128)S(1)} %get-tuple-element.78), channel_id=1, source_target_pairs={{0,2},{1,3},{4,6},{5,7},{8,10},{9,11},{12,14},{13,15},{16,18},{17,... | collective-permute-start | bytes 3145736 | tf_op jit(solution)/shard_map/ppermute | solution.py:185
  36.9 13.9 %all-to-all-start.1 = ((f32[16,40,128]{2,1,0:T(8,128)}), f32[16,40,128]{2,1,0:T(8,128)S(1)}, u32[]{:S(2)}, u32[]{:S(2)}) async-start(f32[16,40,128]{2,1,0:T(8,128)} %broadcast_in_dim.17), calls=%async_computation.1 | async-start | bytes 655360 | tf_op jit(solution)/shard_map/all_to_all | solution.py:236
  41.6 38.0 %collective-permute-start.3 = (f32[512,512]{1,0:T(8,128)}, f32[512,512]{1,0:T(8,128)}, u32[]{:S(2)}, u32[]{:S(2)}) collective-permute-start(f32[512,512]{1,0:T(8,128)} %get-tuple-element.77), channel_id=1, source_target_pairs={{0,2},{1,3},{4,6},{5,7},{8,10},{9,11},{12,14},{13,15},{16,18},{17,... | collective-permute-start | bytes 3145736 | tf_op jit(solution)/shard_map/ppermute | solution.py:185
  49.9 125.4 %copy-start = (f32[512,512]{1,0:T(8,128)}, f32[512,512]{1,0:T(8,128)S(1)}, u32[]{:S(2)}) copy-start(f32[512,512]{1,0:T(8,128)S(1)} %broadcast_select_fusion.5.refs_6_) | copy-start | bytes 3145732
  49.9 30.9 %collective-permute-start.2 = (f32[512,512]{1,0:T(8,128)S(1)}, f32[512,512]{1,0:T(8,128)}, u32[]{:S(2)}, u32[]{:S(2)}) collective-permute-start(f32[512,512]{1,0:T(8,128)S(1)} %broadcast_select_fusion.5.refs_6_), channel_id=1, source_target_pairs={{0,8},{1,9},{2,10},{3,11},{4,12},{5,13},{6,14},{7,15},{8,0},{9,1},... | collective-permute-start | bytes 3145736 | tf_op jit(solution)/shard_map/ppermute | solution.py:185
  50.8 7.7 %collective-permute-start = (f32[16,40,128]{2,1,0:T(8,128)S(1)}, f32[16,40,128]{2,1,0:T(8,128)}, u32[]{:S(2)}, u32[]{:S(2)}) collective-permute-start(f32[16,40,128]{2,1,0:T(8,128)S(1)} %all-to-all-done.1), channel_id=1, source_target_pairs={{0,1},{1,0},{2,3},{3,2},{4,5},{5,4},{6,7},{7,6},{8,9},{9,8},{10,11... | collective-permute-start | bytes 983048 | tf_op jit(solution)/shard_map/ppermute | solution.py:185
  53.9 35.7 %all-to-all-start.2 = ((f32[16,104,128]{2,1,0:T(8,128)}), f32[16,104,128]{2,1,0:T(8,128)S(1)}, u32[]{:S(2)}, u32[]{:S(2)}) async-start(f32[16,104,128]{2,1,0:T(8,128)} %broadcast_in_dim.18), calls=%async_computation.2 | async-start | bytes 1703936 | tf_op jit(solution)/shard_map/all_to_all | solution.py:236
  83.2 27.2 %collective-permute-start.5 = (f32[512,512]{1,0:T(8,128)}, f32[512,512]{1,0:T(8,128)}, u32[]{:S(2)}, u32[]{:S(2)}) collective-permute-start(f32[512,512]{1,0:T(8,128)} %broadcast_select_fusion.3.refs_10_), channel_id=1, source_target_pairs={{8,16},{9,17},{10,18},{11,19},{12,20},{13,21},{14,22},{15,23},{16,... | collective-permute-start | bytes 3145736 | tf_op jit(solution)/shard_map/ppermute | solution.py:185
  86.6 61.9 %copy-start.1 = (f32[512,512]{1,0:T(8,128)}, f32[512,512]{1,0:T(8,128)S(1)}, u32[]{:S(2)}) copy-start(f32[512,512]{1,0:T(8,128)S(1)} %broadcast_select_fusion.4.refs_7_) | copy-start | bytes 3145732
  86.6 23.8 %collective-permute-start.4 = (f32[512,512]{1,0:T(8,128)S(1)}, f32[512,512]{1,0:T(8,128)}, u32[]{:S(2)}, u32[]{:S(2)}) collective-permute-start(f32[512,512]{1,0:T(8,128)S(1)} %broadcast_select_fusion.4.refs_7_), channel_id=1, source_target_pairs={{0,8},{1,9},{2,10},{3,11},{4,12},{5,13},{6,14},{7,15},{8,0},{9,1},... | collective-permute-start | bytes 3145736 | tf_op jit(solution)/shard_map/ppermute | solution.py:185
  88.4 60.1 %collective-permute-start.9 = (f32[512,512]{1,0:T(8,128)}, f32[512,512]{1,0:T(8,128)}, u32[]{:S(2)}, u32[]{:S(2)}) collective-permute-start(f32[512,512]{1,0:T(8,128)} %broadcast_select_fusion.3.refs_10_), channel_id=1, source_target_pairs={{0,4},{1,5},{2,6},{3,7},{4,0},{5,1},{6,2},{7,3},{8,12},{9,13},{10,... | collective-permute-start | bytes 3145736 | tf_op jit(solution)/shard_map/ppermute | solution.py:185
  89.6 20.9 %collective-permute-start.6 = (f32[16,104,128]{2,1,0:T(8,128)S(1)}, f32[16,104,128]{2,1,0:T(8,128)}, u32[]{:S(2)}, u32[]{:S(2)}) collective-permute-start(f32[16,104,128]{2,1,0:T(8,128)S(1)} %all-to-all-done.2), channel_id=1, source_target_pairs={{0,1},{1,0},{2,3},{3,2},{4,5},{5,4},{6,7},{7,6},{8,9},{9,8},{10,11... | collective-permute-start | bytes 2555912 | tf_op jit(solution)/shard_map/ppermute | solution.py:185
  114.4 34.1 %collective-permute-start.8 = (f32[512,512]{1,0:T(8,128)}, f32[512,512]{1,0:T(8,128)}, u32[]{:S(2)}, u32[]{:S(2)}) collective-permute-start(f32[512,512]{1,0:T(8,128)} %broadcast_select_fusion.2.refs_18_), channel_id=1, source_target_pairs={{8,16},{9,17},{10,18},{11,19},{12,20},{13,21},{14,22},{15,23},{16,... | collective-permute-start | bytes 3145736 | tf_op jit(solution)/shard_map/ppermute | solution.py:185
  116.1 34.6 %collective-permute-start.12 = (f32[512,512]{1,0:T(8,128)}, f32[512,512]{1,0:T(8,128)}, u32[]{:S(2)}, u32[]{:S(2)}) collective-permute-start(f32[512,512]{1,0:T(8,128)} %broadcast_select_fusion.2.refs_18_), channel_id=1, source_target_pairs={{0,4},{1,5},{2,6},{3,7},{4,0},{5,1},{6,2},{7,3},{8,12},{9,13},{10,... | collective-permute-start | bytes 3145736 | tf_op jit(solution)/shard_map/ppermute | solution.py:185
  118.6 30.3 %collective-permute-start.7 = (f32[512,512]{1,0:T(8,128)}, f32[512,512]{1,0:T(8,128)}, u32[]{:S(2)}, u32[]{:S(2)}) collective-permute-start(f32[512,512]{1,0:T(8,128)} %collective-permute-done.5), channel_id=1, source_target_pairs={{0,8},{1,9},{2,10},{3,11},{4,12},{5,13},{6,14},{7,15},{8,0},{9,1},... | collective-permute-start | bytes 3145736 | tf_op jit(solution)/shard_map/ppermute | solution.py:185
  144.9 31.7 %collective-permute-start.21 = (f32[512,512]{1,0:T(8,128)}, f32[512,512]{1,0:T(8,128)}, u32[]{:S(2)}, u32[]{:S(2)}) collective-permute-start(f32[512,512]{1,0:T(8,128)} %broadcast_select_fusion.2.refs_18_), channel_id=1, source_target_pairs={{0,1},{1,0},{2,3},{3,2},{4,5},{5,4},{6,7},{7,6},{8,9},{9,8},{10,11... | collective-permute-start | bytes 3145736 | tf_op jit(solution)/shard_map/ppermute | solution.py:185
  148.4 28.3 %collective-permute-start.17 = (f32[512,512]{1,0:T(8,128)}, f32[512,512]{1,0:T(8,128)}, u32[]{:S(2)}, u32[]{:S(2)}) collective-permute-start(f32[512,512]{1,0:T(8,128)} %broadcast_select_fusion.3.refs_10_), channel_id=1, source_target_pairs={{0,1},{1,0},{2,3},{3,2},{4,5},{5,4},{6,7},{7,6},{8,9},{9,8},{10,11... | collective-permute-start | bytes 3145736 | tf_op jit(solution)/shard_map/ppermute | solution.py:185
  148.5 28.6 %collective-permute-start.16 = (f32[512,512]{1,0:T(8,128)S(1)}, f32[512,512]{1,0:T(8,128)}, u32[]{:S(2)}, u32[]{:S(2)}) collective-permute-start(f32[512,512]{1,0:T(8,128)S(1)} %broadcast_select_fusion.4.refs_7_), channel_id=1, source_target_pairs={{0,1},{1,0},{2,3},{3,2},{4,5},{5,4},{6,7},{7,6},{8,9},{9,8},{10,11... | collective-permute-start | bytes 3145736 | tf_op jit(solution)/shard_map/ppermute | solution.py:185
  150.4 25.8 %copy-start.2 = (f32[512,512]{1,0:T(8,128)}, f32[512,512]{1,0:T(8,128)S(1)}, u32[]{:S(2)}) copy-start(f32[512,512]{1,0:T(8,128)S(1)} %broadcast_select_fusion.1.refs_14_) | copy-start | bytes 3145732
  150.4 24.8 %collective-permute-start.11 = (f32[512,512]{1,0:T(8,128)S(1)}, f32[512,512]{1,0:T(8,128)}, u32[]{:S(2)}, u32[]{:S(2)}) collective-permute-start(f32[512,512]{1,0:T(8,128)S(1)} %broadcast_select_fusion.1.refs_14_), channel_id=1, source_target_pairs={{0,4},{1,5},{2,6},{3,7},{4,0},{5,1},{6,2},{7,3},{8,12},{9,13},{10,... | collective-permute-start | bytes 3145736 | tf_op jit(solution)/shard_map/ppermute | solution.py:185
  150.7 25.4 %collective-permute-start.10 = (f32[512,512]{1,0:T(8,128)}, f32[512,512]{1,0:T(8,128)}, u32[]{:S(2)}, u32[]{:S(2)}) collective-permute-start(f32[512,512]{1,0:T(8,128)} %collective-permute-done.8), channel_id=1, source_target_pairs={{0,8},{1,9},{2,10},{3,11},{4,12},{5,13},{6,14},{7,15},{8,0},{9,1},... | collective-permute-start | bytes 3145736 | tf_op jit(solution)/shard_map/ppermute | solution.py:185
  175.2 4.1 %collective-permute-start.15 = (f32[512,512]{1,0:T(8,128)S(1)}, f32[512,512]{1,0:T(8,128)}, u32[]{:S(2)}, u32[]{:S(2)}) collective-permute-start(f32[512,512]{1,0:T(8,128)S(1)} %broadcast_select_fusion.5.refs_6_), channel_id=1, source_target_pairs={{0,1},{1,0},{2,3},{3,2},{4,5},{5,4},{6,7},{7,6},{8,9},{9,8},{10,11... | collective-permute-start | bytes 3145736 | tf_op jit(solution)/shard_map/ppermute | solution.py:185
  176.2 4.5 %collective-permute-start.19 = (f32[512,512]{1,0:T(8,128)S(1)}, f32[512,512]{1,0:T(8,128)}, u32[]{:S(2)}, u32[]{:S(2)}) collective-permute-start(f32[512,512]{1,0:T(8,128)S(1)} %broadcast_select_fusion.1.refs_14_), channel_id=1, source_target_pairs={{0,1},{1,0},{2,3},{3,2},{4,5},{5,4},{6,7},{7,6},{8,9},{9,8},{10,11... | collective-permute-start | bytes 3145736 | tf_op jit(solution)/shard_map/ppermute | solution.py:185
  176.6 4.9 %collective-permute-start.18 = (f32[512,512]{1,0:T(8,128)}, f32[512,512]{1,0:T(8,128)}, u32[]{:S(2)}, u32[]{:S(2)}) collective-permute-start(f32[512,512]{1,0:T(8,128)} %collective-permute-done.9.refs_12_), channel_id=1, source_target_pairs={{0,1},{1,0},{2,3},{3,2},{4,5},{5,4},{6,7},{7,6},{8,9},{9,8},{10,11... | collective-permute-start | bytes 3145736 | tf_op jit(solution)/shard_map/ppermute | solution.py:185
  176.7 6.4 %collective-permute-start.20 = (f32[512,512]{1,0:T(8,128)}, f32[512,512]{1,0:T(8,128)}, u32[]{:S(2)}, u32[]{:S(2)}) collective-permute-start(f32[512,512]{1,0:T(8,128)} %collective-permute-done.11.refs_16_), channel_id=1, source_target_pairs={{0,1},{1,0},{2,3},{3,2},{4,5},{5,4},{6,7},{7,6},{8,9},{9,8},{10,11... | collective-permute-start | bytes 3145736 | tf_op jit(solution)/shard_map/ppermute | solution.py:185
  177.2 7.3 %collective-permute-start.22 = (f32[512,512]{1,0:T(8,128)}, f32[512,512]{1,0:T(8,128)S(1)}, u32[]{:S(2)}, u32[]{:S(2)}) collective-permute-start(f32[512,512]{1,0:T(8,128)} %collective-permute-done.12.refs_20_), channel_id=1, source_target_pairs={{0,1},{1,0},{2,3},{3,2},{4,5},{5,4},{6,7},{7,6},{8,9},{9,8},{10,11... | collective-permute-start | bytes 3145736 | tf_op jit(solution)/shard_map/ppermute | solution.py:185
  179.3 37.9 %copy-start.3 = (f32[512,512]{1,0:T(8,128)}, f32[512,512]{1,0:T(8,128)S(1)}, u32[]{:S(2)}) copy-start(f32[512,512]{1,0:T(8,128)S(1)} %broadcast_select_fusion.refs_6_) | copy-start | bytes 3145732
  179.4 37.9 %collective-permute-start.14 = (f32[512,512]{1,0:T(8,128)S(1)}, f32[512,512]{1,0:T(8,128)S(1)}, u32[]{:S(2)}, u32[]{:S(2)}) collective-permute-start(f32[512,512]{1,0:T(8,128)S(1)} %broadcast_select_fusion.refs_6_), channel_id=1, source_target_pairs={{0,4},{1,5},{2,6},{3,7},{4,0},{5,1},{6,2},{7,3},{8,12},{9,13},{10,... | collective-permute-start | bytes 3145736 | tf_op jit(solution)/shard_map/ppermute | solution.py:185
  180.6 37.0 %collective-permute-start.13 = (f32[512,512]{1,0:T(8,128)S(1)}, f32[512,512]{1,0:T(8,128)S(1)}, u32[]{:S(2)}, u32[]{:S(2)}) collective-permute-start(f32[512,512]{1,0:T(8,128)S(1)} %broadcast_select_fusion.refs_6_), channel_id=1, source_target_pairs={{0,1},{1,0},{2,3},{3,2},{4,5},{5,4},{6,7},{7,6},{8,9},{9,8},{10,11... | collective-permute-start | bytes 3145736 | tf_op jit(solution)/shard_map/ppermute | solution.py:185
  184.4 1.0 copy-start.4
  217.2 2.7 %copy-start.5 = (f32[512,512]{1,0:T(8,128)}, f32[512,512]{1,0:T(8,128)S(1)}, u32[]{:S(2)}) copy-start(f32[512,512]{1,0:T(8,128)S(1)} %collective-permute-done.14.refs_8_) | copy-start | bytes 3145732
  217.2 2.7 %collective-permute-start.23 = (f32[512,512]{1,0:T(8,128)S(1)}, f32[512,512]{1,0:T(8,128)S(1)}, u32[]{:S(2)}, u32[]{:S(2)}) collective-permute-start(f32[512,512]{1,0:T(8,128)S(1)} %collective-permute-done.14.refs_8_), channel_id=1, source_target_pairs={{0,1},{1,0},{2,3},{3,2},{4,5},{5,4},{6,7},{7,6},{8,9},{9,8},{10,11... | collective-permute-start | bytes 3145736 | tf_op jit(solution)/shard_map/ppermute | solution.py:185
  217.7 2.3 copy-start.6
  220.0 1.0 copy-start.7

commit v2 on v1

--- a/solution.py
+++ b/solution.py
@@ -265,11 +265,17 @@
     return high, (x - high.astype(jnp.float32)).astype(jnp.bfloat16)
 
 
-def product(a, b, cb):
-    def one(x, y):
-        return lax.dot_general(x, y, (((1,), (cb,)), ((), ())), preferred_element_type=jnp.float32)
-
-    return one(a[0], b[0]) + (one(a[0], b[1]) + one(a[1], b[0]))
+def product(*pairs):
+    left, right = [], []
+    for a, b in pairs:
+        left += [a[0], a[0], a[1]]
+        right += [b[0], b[1], b[0]]
+    return lax.dot_general(
+        jnp.concatenate(left, 1),
+        jnp.concatenate(right, 1),
+        (((1,), (1,)), ((), ())),
+        preferred_element_type=jnp.float32,
+    )
 
 
 def finish_kernel(shape, steps, opening, scalars, *refs):
@@ -339,8 +345,8 @@
     mid = n // 2
 
     def times_lower(x, yh, yl):
-        head = product((x[0][:, :mid], x[1][:, :mid]), (yh[:mid, :mid], yl[:mid, :mid]), 1)
-        return jnp.concatenate([head, product(x, (yh[mid:, :], yl[mid:, :]), 1)], 1)
+        head = product(((x[0][:, :mid], x[1][:, :mid]), (yh[:mid, :mid], yl[:mid, :mid])))
+        return jnp.concatenate([head, product((x, (yh[mid:, :], yl[mid:, :])))], 1)
 
     def solve(k, carry):
         at = k if opening else k + count
@@ -352,7 +358,7 @@
         def strip(c, carry):
             part = pl.ds(pl.multiple_of(c * mid, mid), mid)
             whole = (high[at, 0], low[at, 0])
-            raw[k, 1, :, part] = raw[k, 1, :, part] - product(whole, (lh[part, :], ll[part, :]), 1)
+            raw[k, 1, :, part] = raw[k, 1, :, part] - product((whole, (lh[part, :], ll[part, :])))
             return carry
 
         lax.fori_loop(0, 2, strip, 0)
@@ -402,11 +408,11 @@
         def _():
             def strip(c, carry):
                 at = pl.ds(pl.multiple_of(c * mid, mid), mid)
-                value = gbuf[slot, :, at]
+                pairs = []
                 for panel in range(2):
                     column_part = (high[count + e, panel, at, :], low[count + e, panel, at, :])
-                    value = value - product((high[a, panel], low[a, panel]), column_part, 1)
-                obuf[slot, :, at] = value
+                    pairs.append(((high[a, panel], low[a, panel]), column_part))
+                obuf[slot, :, at] = gbuf[slot, :, at] - product(*pairs)
                 return carry
 
             lax.fori_loop(0, 2, strip, 0)

time: 234 us -> 234 us (level)
  no operation moved by 1% of the time
where the time goes in v2:
time: 234 us; the launch traced here: 233 us
  Pallas kernels  123 us (53%)
  waiting for transfers between devices  43.7 us (19%)
  starting transfers between devices  40.5 us (17%)
  other arithmetic  17.8 us (8%)
  local copies, waits for them, and re-layouts  7.47 us (3%)
    pallas_call x4, Pallas kernels, call(): pl.pallas_call(kernel, out_shape=[jax.ShapeDtypeStruct((size, size), jnp....  79.4 us
    pallas_call x2, Pallas kernels, finish(): pl.pallas_call(functools.partial(finish_kernel, (count, width, n), steps,...  43.2 us
    ppermute x24, starting transfers between devices, send(): return lax.ppermute(x, AXES, pairs)  24.9 us
    all_to_all x1, waiting for transfers between devices, scatter(): got = lax.all_to_all(jnp.concatenate(parts, 1), AXES, 0, 0, tiled=True)  24.4 us
    ppermute x24, waiting for transfers between devices, send(): return lax.ppermute(x, AXES, pairs)  18.4 us
    all_to_all x2, starting transfers between devices, gather(): mine = lax.all_to_all(spread, ('row', 'y'), 0, 0, tiled=True)  9.28 us
    all_to_all x1, starting transfers between devices, scatter(): got = lax.all_to_all(jnp.concatenate(parts, 1), AXES, 0, 0, tiled=True)  6.38 us
    select_n x2, other arithmetic, pair_finish(): same = jnp.where(grid.hi % grid.ys ^ grid.y == s, got[s - 1], same)  4.97 us
  transfers between devices with their start and end apart: 27, of which 9 were waited for; matrix products, arithmetic and copies ran while one was open for 8% of the time, Pallas kernels for 48%

profile of v2, /device:TPU:5, one launch (start us, length us, event | category | flops | bytes accessed | tf_op | source)
XLA Modules:
  0.0 232.5 jit_solution(12664772965964968645)
XLA Ops:
  0.0 2.7 %slice_bitcast_fusion = (f32[512,512]{1,0:T(8,128)}, f32[512,512]{1,0:T(8,128)S(1)}) fusion(f32[2,4,512,512]{3,2,1,0:T(8,128)} %bitcast.184), kind=kLoop, calls=%fused_computation.11 | loop fusion | bytes 4194304 | tf_op jit(solution)/shard_map/squeeze | solution.py:513
  2.9 1.1 pad_maximum_fusion.5
  4.0 6.4 %all-to-all-start = ((f32[32,64,128]{2,1,0:T(8,128)}), f32[32,64,128]{2,1,0:T(8,128)S(1)}, u32[]{:S(2)}, u32[]{:S(2)}) async-start(f32[32,64,128]{2,1,0:T(8,128)} %pad_maximum_fusion.5), calls=%async_computation | async-start | bytes 2097152 | tf_op jit(solution)/shard_map/all_to_all | solution.py:229
  10.4 1.3 collective-permute-start.1
  11.7 24.4 %all-to-all-done = f32[32,64,128]{2,1,0:T(8,128)S(1)} async-done(((f32[32,64,128]{2,1,0:T(8,128)}), f32[32,64,128]{2,1,0:T(8,128)S(1)}, u32[]{:S(2)}, u32[]{:S(2)}) %all-to-all-start) | async-done | bytes 1048608 | tf_op jit(solution)/shard_map/all_to_all | solution.py:229
  36.1 0.8 broadcast_in_dim.17
  36.9 4.7 %all-to-all-start.1 = ((f32[16,40,128]{2,1,0:T(8,128)}), f32[16,40,128]{2,1,0:T(8,128)S(1)}, u32[]{:S(2)}, u32[]{:S(2)}) async-start(f32[16,40,128]{2,1,0:T(8,128)} %broadcast_in_dim.17), calls=%async_computation.1 | async-start | bytes 655360 | tf_op jit(solution)/shard_map/all_to_all | solution.py:236
  41.6 1.3 collective-permute-start.3
  42.9 5.5 %collective-permute-done.1 = f32[512,512]{1,0:T(8,128)S(1)} collective-permute-done((f32[512,512]{1,0:T(8,128)S(1)}, f32[512,512]{1,0:T(8,128)S(1)}, u32[]{:S(2)}, u32[]{:S(2)}) %collective-permute-start.1) | collective-permute-done | bytes 1048608 | tf_op jit(solution)/shard_map/ppermute | solution.py:185
  48.4 1.4 broadcast_select_fusion.5.refs_6_
  49.9 0.8 all-to-all-done.1
  50.8 2.1 collective-permute-start
  52.9 1.0 broadcast_in_dim.18
  53.9 4.6 %all-to-all-start.2 = ((f32[16,104,128]{2,1,0:T(8,128)}), f32[16,104,128]{2,1,0:T(8,128)S(1)}, u32[]{:S(2)}, u32[]{:S(2)}) async-start(f32[16,104,128]{2,1,0:T(8,128)} %broadcast_in_dim.18), calls=%async_computation.2 | async-start | bytes 1703936 | tf_op jit(solution)/shard_map/all_to_all | solution.py:236
  58.5 1.0 select_bitcast_fusion.3
  59.6 1.1 fusion.2.x_ref
  60.7 18.8 %shard_map.17 = (f32[256,256]{1,0:T(8,128)}, f32[512,512]{1,0:T(8,128)}, f32[512,512]{1,0:T(8,128)}) custom-call(f32[512,512]{1,0:T(8,128)} %fusion.2.x_ref), custom_call_target="tpu_custom_call" | custom-call | flops 20000000000 | bytes 60000000 | tf_op jit(solution)/shard_map/pallas_call | solution.py:133
  79.5 1.2 collective-permute-done.2
  80.7 2.5 %broadcast_select_fusion.3.refs_10_ = f32[512,512]{1,0:T(8,128)} fusion(f32[512,512]{1,0:T(8,128)} %collective-permute-done.2, f32[512,512]{1,0:T(8,128)S(1)} %broadcast_select_fusion.5.refs_6_, pred[]{:T(512)S(6)} %eq.41), kind=kLoop, calls=%fused_computation.22 | loop fusion | flops 262144 | bytes 3145729 | tf_op jit(solution)/shard_map/jit(_where)/select_n | solution.py:530
  83.2 1.6 collective-permute-start.5
  84.9 1.7 broadcast_select_fusion.4.refs_7_
  86.6 1.8 collective-permute-start.4
  88.4 1.2 collective-permute-start.9
  89.6 2.6 %collective-permute-start.6 = (f32[16,104,128]{2,1,0:T(8,128)S(1)}, f32[16,104,128]{2,1,0:T(8,128)}, u32[]{:S(2)}, u32[]{:S(2)}) collective-permute-start(f32[16,104,128]{2,1,0:T(8,128)S(1)} %all-to-all-done.2), channel_id=1, source_target_pairs={{0,1},{1,0},{2,3},{3,2},{4,5},{5,4},{6,7},{7,6},{8,9},{9,8},{10,11... | collective-permute-start | bytes 2555912 | tf_op jit(solution)/shard_map/ppermute | solution.py:185
  92.2 18.2 %shard_map.18 = (f32[512,512]{1,0:T(8,128)}, f32[512,512]{1,0:T(8,128)}) custom-call(f32[256,256]{1,0:T(8,128)} %get-tuple-element.45.rest_ref, f32[512,512]{1,0:T(8,128)} %get-tuple-element.46.l_in, f32[512,512]{1,0:T(8,128)} %get-tuple-element.47.w_in), custom_call_target="tpu_custom_call" | custom-call | flops 20000000000 | bytes 60000000 | tf_op jit(solution)/shard_map/pallas_call | solution.py:133
  110.4 1.3 select_bitcast_fusion.1
  112.0 2.5 %broadcast_select_fusion.2.refs_18_ = f32[512,512]{1,0:T(8,128)} fusion(f32[512,512]{1,0:T(8,128)} %collective-permute-done.4, f32[512,512]{1,0:T(8,128)S(1)} %broadcast_select_fusion.4.refs_7_, pred[]{:T(512)S(6)} %eq.41), kind=kLoop, calls=%fused_computation.21 | loop fusion | flops 262144 | bytes 3145729 | tf_op jit(solution)/shard_map/jit(_where)/select_n | solution.py:530
  114.4 1.7 collective-permute-start.8
  116.1 1.3 collective-permute-start.12
  117.6 1.0 maximum_maximum_fusion.side_ref
  118.6 1.1 collective-permute-start.7
  119.8 1.1 fusion.5.x_ref
  120.8 24.1 %shard_map.19 = (f32[512,512]{1,0:T(8,128)}, f32[256,256]{1,0:T(8,128)}, f32[512,512]{1,0:T(8,128)}, f32[512,512]{1,0:T(8,128)}) custom-call(f32[512,512]{1,0:T(8,128)} %maximum_maximum_fusion.side_ref, f32[512,512]{1,0:T(8,128)} %fusion.5.x_ref, f32[512,512]{1,0:T(8,128)} %get-tuple-element.49.inverse_ref.refs_4_), custom_call_target="tpu_custom_call" | custom-call | flops 20000000000 | bytes 60000000 | tf_op jit(solution)/shard_map/pallas_call | solution.py:133
  144.9 3.5 %collective-permute-start.21 = (f32[512,512]{1,0:T(8,128)}, f32[512,512]{1,0:T(8,128)}, u32[]{:S(2)}, u32[]{:S(2)}) collective-permute-start(f32[512,512]{1,0:T(8,128)} %broadcast_select_fusion.2.refs_18_), channel_id=1, source_target_pairs={{0,1},{1,0},{2,3},{3,2},{4,5},{5,4},{6,7},{7,6},{8,9},{9,8},{10,11... | collective-permute-start | bytes 3145736 | tf_op jit(solution)/shard_map/ppermute | solution.py:185
  149.0 1.4 broadcast_select_fusion.1.refs_14_
  150.8 18.2 %shard_map.20 = (f32[512,512]{1,0:T(8,128)}, f32[512,512]{1,0:T(8,128)}) custom-call(f32[256,256]{1,0:T(8,128)} %get-tuple-element.58.rest_ref, f32[512,512]{1,0:T(8,128)} %get-tuple-element.59.l_in, f32[512,512]{1,0:T(8,128)} %get-tuple-element.60.w_in), custom_call_target="tpu_custom_call" | custom-call | flops 20000000000 | bytes 60000000 | tf_op jit(solution)/shard_map/pallas_call | solution.py:133
  168.9 6.3 %collective-permute-done.11.refs_16_ = f32[512,512]{1,0:T(8,128)} collective-permute-done((f32[512,512]{1,0:T(8,128)S(1)}, f32[512,512]{1,0:T(8,128)}, u32[]{:S(2)}, u32[]{:S(2)}) %collective-permute-start.11) | collective-permute-done | bytes 1048608 | tf_op jit(solution)/shard_map/ppermute | solution.py:185
  175.2 0.9 collective-permute-start.15
  177.9 1.4 broadcast_select_fusion.refs_6_
  179.4 1.3 collective-permute-start.14
  180.6 0.7 collective-permute-start.13
  181.6 1.5 collective-permute-done.20.refs_17_
  183.1 1.4 collective-permute-done.22.refs_21_
  184.5 1.0 copy-done.4
  185.4 31.8 %shard_map.21 = (f32[2,4,512,512]{3,2,1,0:T(8,128)}, bf16[2,2,512,512]{3,2,1,0:T(8,128)(2,1)}, bf16[2,2,512,512]{3,2,1,0:T(8,128)(2,1)}) custom-call(s32[6]{0:T(128)} %stack.118.scalars, f32[2,4,512,512]{3,2,1,0:T(8,128)} %bitcast.187, f32[512,512]{1,0:T(8,128)} %get-tuple-element.48.refs_1_, f32[512,512]{1,0:T(8,128)} %get-tuple-element.54.refs_2_, ...), custom_call_target="tpu_custom_call" | custom-call | flops 20000000000 | bytes 60000000 | tf_op jit(solution)/shard_map/pallas_call | solution.py:479
  217.7 2.3 collective-permute-done.23.refs_9_
  220.0 0.9 copy-done.7
  220.9 11.4 %shard_map.22 = f32[2,4,512,512]{3,2,1,0:T(8,128)} custom-call(s32[6]{0:T(128)} %stack.118.scalars, f32[2,4,512,512]{3,2,1,0:T(8,128)} %bitcast.188, f32[512,512]{1,0:T(8,128)} %get-tuple-element.48.refs_1_, f32[512,512]{1,0:T(8,128)} %get-tuple-element.54.refs_2_, f32[512,512]{1,0:T(8,128)} %get-tuple-element.61.refs_3_, ...), custom_call_target="tpu_custom_call", output_to_operand_aliasing={{}: (11, {})} | custom-call | flops 20000000000 | bytes 60000000 | tf_op jit(solution)/shard_map/pallas_call | solution.py:479
  (66 shorter events, 4.0 us)
Async XLA Ops:
  4.0 32.1 %all-to-all-start = ((f32[32,64,128]{2,1,0:T(8,128)}), f32[32,64,128]{2,1,0:T(8,128)S(1)}, u32[]{:S(2)}, u32[]{:S(2)}) async-start(f32[32,64,128]{2,1,0:T(8,128)} %pad_maximum_fusion.5), calls=%async_computation | async-start | bytes 2097152 | tf_op jit(solution)/shard_map/all_to_all | solution.py:229
  10.4 38.0 %collective-permute-start.1 = (f32[512,512]{1,0:T(8,128)S(1)}, f32[512,512]{1,0:T(8,128)S(1)}, u32[]{:S(2)}, u32[]{:S(2)}) collective-permute-start(f32[512,512]{1,0:T(8,128)S(1)} %get-tuple-element.78), channel_id=1, source_target_pairs={{0,2},{1,3},{4,6},{5,7},{8,10},{9,11},{12,14},{13,15},{16,18},{17,... | collective-permute-start | bytes 3145736 | tf_op jit(solution)/shard_map/ppermute | solution.py:185
  36.9 13.9 %all-to-all-start.1 = ((f32[16,40,128]{2,1,0:T(8,128)}), f32[16,40,128]{2,1,0:T(8,128)S(1)}, u32[]{:S(2)}, u32[]{:S(2)}) async-start(f32[16,40,128]{2,1,0:T(8,128)} %broadcast_in_dim.17), calls=%async_computation.1 | async-start | bytes 655360 | tf_op jit(solution)/shard_map/all_to_all | solution.py:236
  41.6 38.0 %collective-permute-start.3 = (f32[512,512]{1,0:T(8,128)}, f32[512,512]{1,0:T(8,128)}, u32[]{:S(2)}, u32[]{:S(2)}) collective-permute-start(f32[512,512]{1,0:T(8,128)} %get-tuple-element.77), channel_id=1, source_target_pairs={{0,2},{1,3},{4,6},{5,7},{8,10},{9,11},{12,14},{13,15},{16,18},{17,... | collective-permute-start | bytes 3145736 | tf_op jit(solution)/shard_map/ppermute | solution.py:185
  49.9 125.4 %copy-start = (f32[512,512]{1,0:T(8,128)}, f32[512,512]{1,0:T(8,128)S(1)}, u32[]{:S(2)}) copy-start(f32[512,512]{1,0:T(8,128)S(1)} %broadcast_select_fusion.5.refs_6_) | copy-start | bytes 3145732
  49.9 30.9 %collective-permute-start.2 = (f32[512,512]{1,0:T(8,128)S(1)}, f32[512,512]{1,0:T(8,128)}, u32[]{:S(2)}, u32[]{:S(2)}) collective-permute-start(f32[512,512]{1,0:T(8,128)S(1)} %broadcast_select_fusion.5.refs_6_), channel_id=1, source_target_pairs={{0,8},{1,9},{2,10},{3,11},{4,12},{5,13},{6,14},{7,15},{8,0},{9,1},... | collective-permute-start | bytes 3145736 | tf_op jit(solution)/shard_map/ppermute | solution.py:185
  50.8 7.7 %collective-permute-start = (f32[16,40,128]{2,1,0:T(8,128)S(1)}, f32[16,40,128]{2,1,0:T(8,128)}, u32[]{:S(2)}, u32[]{:S(2)}) collective-permute-start(f32[16,40,128]{2,1,0:T(8,128)S(1)} %all-to-all-done.1), channel_id=1, source_target_pairs={{0,1},{1,0},{2,3},{3,2},{4,5},{5,4},{6,7},{7,6},{8,9},{9,8},{10,11... | collective-permute-start | bytes 983048 | tf_op jit(solution)/shard_map/ppermute | solution.py:185
  53.9 35.7 %all-to-all-start.2 = ((f32[16,104,128]{2,1,0:T(8,128)}), f32[16,104,128]{2,1,0:T(8,128)S(1)}, u32[]{:S(2)}, u32[]{:S(2)}) async-start(f32[16,104,128]{2,1,0:T(8,128)} %broadcast_in_dim.18), calls=%async_computation.2 | async-start | bytes 1703936 | tf_op jit(solution)/shard_map/all_to_all | solution.py:236
  83.2 27.2 %collective-permute-start.5 = (f32[512,512]{1,0:T(8,128)}, f32[512,512]{1,0:T(8,128)}, u32[]{:S(2)}, u32[]{:S(2)}) collective-permute-start(f32[512,512]{1,0:T(8,128)} %broadcast_select_fusion.3.refs_10_), channel_id=1, source_target_pairs={{8,16},{9,17},{10,18},{11,19},{12,20},{13,21},{14,22},{15,23},{16,... | collective-permute-start | bytes 3145736 | tf_op jit(solution)/shard_map/ppermute | solution.py:185
  86.6 61.9 %copy-start.1 = (f32[512,512]{1,0:T(8,128)}, f32[512,512]{1,0:T(8,128)S(1)}, u32[]{:S(2)}) copy-start(f32[512,512]{1,0:T(8,128)S(1)} %broadcast_select_fusion.4.refs_7_) | copy-start | bytes 3145732
  86.6 23.8 %collective-permute-start.4 = (f32[512,512]{1,0:T(8,128)S(1)}, f32[512,512]{1,0:T(8,128)}, u32[]{:S(2)}, u32[]{:S(2)}) collective-permute-start(f32[512,512]{1,0:T(8,128)S(1)} %broadcast_select_fusion.4.refs_7_), channel_id=1, source_target_pairs={{0,8},{1,9},{2,10},{3,11},{4,12},{5,13},{6,14},{7,15},{8,0},{9,1},... | collective-permute-start | bytes 3145736 | tf_op jit(solution)/shard_map/ppermute | solution.py:185
  88.4 60.1 %collective-permute-start.9 = (f32[512,512]{1,0:T(8,128)}, f32[512,512]{1,0:T(8,128)}, u32[]{:S(2)}, u32[]{:S(2)}) collective-permute-start(f32[512,512]{1,0:T(8,128)} %broadcast_select_fusion.3.refs_10_), channel_id=1, source_target_pairs={{0,4},{1,5},{2,6},{3,7},{4,0},{5,1},{6,2},{7,3},{8,12},{9,13},{10,... | collective-permute-start | bytes 3145736 | tf_op jit(solution)/shard_map/ppermute | solution.py:185
  89.6 20.9 %collective-permute-start.6 = (f32[16,104,128]{2,1,0:T(8,128)S(1)}, f32[16,104,128]{2,1,0:T(8,128)}, u32[]{:S(2)}, u32[]{:S(2)}) collective-permute-start(f32[16,104,128]{2,1,0:T(8,128)S(1)} %all-to-all-done.2), channel_id=1, source_target_pairs={{0,1},{1,0},{2,3},{3,2},{4,5},{5,4},{6,7},{7,6},{8,9},{9,8},{10,11... | collective-permute-start | bytes 2555912 | tf_op jit(solution)/shard_map/ppermute | solution.py:185
  114.4 34.1 %collective-permute-start.8 = (f32[512,512]{1,0:T(8,128)}, f32[512,512]{1,0:T(8,128)}, u32[]{:S(2)}, u32[]{:S(2)}) collective-permute-start(f32[512,512]{1,0:T(8,128)} %broadcast_select_fusion.2.refs_18_), channel_id=1, source_target_pairs={{8,16},{9,17},{10,18},{11,19},{12,20},{13,21},{14,22},{15,23},{16,... | collective-permute-start | bytes 3145736 | tf_op jit(solution)/shard_map/ppermute | solution.py:185
  116.1 34.6 %collective-permute-start.12 = (f32[512,512]{1,0:T(8,128)}, f32[512,512]{1,0:T(8,128)}, u32[]{:S(2)}, u32[]{:S(2)}) collective-permute-start(f32[512,512]{1,0:T(8,128)} %broadcast_select_fusion.2.refs_18_), channel_id=1, source_target_pairs={{0,4},{1,5},{2,6},{3,7},{4,0},{5,1},{6,2},{7,3},{8,12},{9,13},{10,... | collective-permute-start | bytes 3145736 | tf_op jit(solution)/shard_map/ppermute | solution.py:185
  118.6 30.3 %collective-permute-start.7 = (f32[512,512]{1,0:T(8,128)}, f32[512,512]{1,0:T(8,128)}, u32[]{:S(2)}, u32[]{:S(2)}) collective-permute-start(f32[512,512]{1,0:T(8,128)} %collective-permute-done.5), channel_id=1, source_target_pairs={{0,8},{1,9},{2,10},{3,11},{4,12},{5,13},{6,14},{7,15},{8,0},{9,1},... | collective-permute-start | bytes 3145736 | tf_op jit(solution)/shard_map/ppermute | solution.py:185
  144.9 31.7 %collective-permute-start.21 = (f32[512,512]{1,0:T(8,128)}, f32[512,512]{1,0:T(8,128)}, u32[]{:S(2)}, u32[]{:S(2)}) collective-permute-start(f32[512,512]{1,0:T(8,128)} %broadcast_select_fusion.2.refs_18_), channel_id=1, source_target_pairs={{0,1},{1,0},{2,3},{3,2},{4,5},{5,4},{6,7},{7,6},{8,9},{9,8},{10,11... | collective-permute-start | bytes 3145736 | tf_op jit(solution)/shard_map/ppermute | solution.py:185
  148.4 28.3 %collective-permute-start.17 = (f32[512,512]{1,0:T(8,128)}, f32[512,512]{1,0:T(8,128)}, u32[]{:S(2)}, u32[]{:S(2)}) collective-permute-start(f32[512,512]{1,0:T(8,128)} %broadcast_select_fusion.3.refs_10_), channel_id=1, source_target_pairs={{0,1},{1,0},{2,3},{3,2},{4,5},{5,4},{6,7},{7,6},{8,9},{9,8},{10,11... | collective-permute-start | bytes 3145736 | tf_op jit(solution)/shard_map/ppermute | solution.py:185
  148.5 28.6 %collective-permute-start.16 = (f32[512,512]{1,0:T(8,128)S(1)}, f32[512,512]{1,0:T(8,128)}, u32[]{:S(2)}, u32[]{:S(2)}) collective-permute-start(f32[512,512]{1,0:T(8,128)S(1)} %broadcast_select_fusion.4.refs_7_), channel_id=1, source_target_pairs={{0,1},{1,0},{2,3},{3,2},{4,5},{5,4},{6,7},{7,6},{8,9},{9,8},{10,11... | collective-permute-start | bytes 3145736 | tf_op jit(solution)/shard_map/ppermute | solution.py:185
  150.4 25.8 %copy-start.2 = (f32[512,512]{1,0:T(8,128)}, f32[512,512]{1,0:T(8,128)S(1)}, u32[]{:S(2)}) copy-start(f32[512,512]{1,0:T(8,128)S(1)} %broadcast_select_fusion.1.refs_14_) | copy-start | bytes 3145732
  150.4 24.8 %collective-permute-start.11 = (f32[512,512]{1,0:T(8,128)S(1)}, f32[512,512]{1,0:T(8,128)}, u32[]{:S(2)}, u32[]{:S(2)}) collective-permute-start(f32[512,512]{1,0:T(8,128)S(1)} %broadcast_select_fusion.1.refs_14_), channel_id=1, source_target_pairs={{0,4},{1,5},{2,6},{3,7},{4,0},{5,1},{6,2},{7,3},{8,12},{9,13},{10,... | collective-permute-start | bytes 3145736 | tf_op jit(solution)/shard_map/ppermute | solution.py:185
  150.7 25.4 %collective-permute-start.10 = (f32[512,512]{1,0:T(8,128)}, f32[512,512]{1,0:T(8,128)}, u32[]{:S(2)}, u32[]{:S(2)}) collective-permute-start(f32[512,512]{1,0:T(8,128)} %collective-permute-done.8), channel_id=1, source_target_pairs={{0,8},{1,9},{2,10},{3,11},{4,12},{5,13},{6,14},{7,15},{8,0},{9,1},... | collective-permute-start | bytes 3145736 | tf_op jit(solution)/shard_map/ppermute | solution.py:185
  175.2 4.1 %collective-permute-start.15 = (f32[512,512]{1,0:T(8,128)S(1)}, f32[512,512]{1,0:T(8,128)}, u32[]{:S(2)}, u32[]{:S(2)}) collective-permute-start(f32[512,512]{1,0:T(8,128)S(1)} %broadcast_select_fusion.5.refs_6_), channel_id=1, source_target_pairs={{0,1},{1,0},{2,3},{3,2},{4,5},{5,4},{6,7},{7,6},{8,9},{9,8},{10,11... | collective-permute-start | bytes 3145736 | tf_op jit(solution)/shard_map/ppermute | solution.py:185
  176.2 4.5 %collective-permute-start.19 = (f32[512,512]{1,0:T(8,128)S(1)}, f32[512,512]{1,0:T(8,128)}, u32[]{:S(2)}, u32[]{:S(2)}) collective-permute-start(f32[512,512]{1,0:T(8,128)S(1)} %broadcast_select_fusion.1.refs_14_), channel_id=1, source_target_pairs={{0,1},{1,0},{2,3},{3,2},{4,5},{5,4},{6,7},{7,6},{8,9},{9,8},{10,11... | collective-permute-start | bytes 3145736 | tf_op jit(solution)/shard_map/ppermute | solution.py:185
  176.6 4.9 %collective-permute-start.18 = (f32[512,512]{1,0:T(8,128)}, f32[512,512]{1,0:T(8,128)}, u32[]{:S(2)}, u32[]{:S(2)}) collective-permute-start(f32[512,512]{1,0:T(8,128)} %collective-permute-done.9.refs_12_), channel_id=1, source_target_pairs={{0,1},{1,0},{2,3},{3,2},{4,5},{5,4},{6,7},{7,6},{8,9},{9,8},{10,11... | collective-permute-start | bytes 3145736 | tf_op jit(solution)/shard_map/ppermute | solution.py:185
  176.7 6.4 %collective-permute-start.20 = (f32[512,512]{1,0:T(8,128)}, f32[512,512]{1,0:T(8,128)}, u32[]{:S(2)}, u32[]{:S(2)}) collective-permute-start(f32[512,512]{1,0:T(8,128)} %collective-permute-done.11.refs_16_), channel_id=1, source_target_pairs={{0,1},{1,0},{2,3},{3,2},{4,5},{5,4},{6,7},{7,6},{8,9},{9,8},{10,11... | collective-permute-start | bytes 3145736 | tf_op jit(solution)/shard_map/ppermute | solution.py:185
  177.2 7.3 %collective-permute-start.22 = (f32[512,512]{1,0:T(8,128)}, f32[512,512]{1,0:T(8,128)S(1)}, u32[]{:S(2)}, u32[]{:S(2)}) collective-permute-start(f32[512,512]{1,0:T(8,128)} %collective-permute-done.12.refs_20_), channel_id=1, source_target_pairs={{0,1},{1,0},{2,3},{3,2},{4,5},{5,4},{6,7},{7,6},{8,9},{9,8},{10,11... | collective-permute-start | bytes 3145736 | tf_op jit(solution)/shard_map/ppermute | solution.py:185
  179.3 37.9 %copy-start.3 = (f32[512,512]{1,0:T(8,128)}, f32[512,512]{1,0:T(8,128)S(1)}, u32[]{:S(2)}) copy-start(f32[512,512]{1,0:T(8,128)S(1)} %broadcast_select_fusion.refs_6_) | copy-start | bytes 3145732
  179.4 37.8 %collective-permute-start.14 = (f32[512,512]{1,0:T(8,128)S(1)}, f32[512,512]{1,0:T(8,128)S(1)}, u32[]{:S(2)}, u32[]{:S(2)}) collective-permute-start(f32[512,512]{1,0:T(8,128)S(1)} %broadcast_select_fusion.refs_6_), channel_id=1, source_target_pairs={{0,4},{1,5},{2,6},{3,7},{4,0},{5,1},{6,2},{7,3},{8,12},{9,13},{10,... | collective-permute-start | bytes 3145736 | tf_op jit(solution)/shard_map/ppermute | solution.py:185
  180.6 37.1 %collective-permute-start.13 = (f32[512,512]{1,0:T(8,128)S(1)}, f32[512,512]{1,0:T(8,128)S(1)}, u32[]{:S(2)}, u32[]{:S(2)}) collective-permute-start(f32[512,512]{1,0:T(8,128)S(1)} %broadcast_select_fusion.refs_6_), channel_id=1, source_target_pairs={{0,1},{1,0},{2,3},{3,2},{4,5},{5,4},{6,7},{7,6},{8,9},{9,8},{10,11... | collective-permute-start | bytes 3145736 | tf_op jit(solution)/shard_map/ppermute | solution.py:185
  184.4 1.0 copy-start.4
  217.2 2.8 %copy-start.5 = (f32[512,512]{1,0:T(8,128)}, f32[512,512]{1,0:T(8,128)S(1)}, u32[]{:S(2)}) copy-start(f32[512,512]{1,0:T(8,128)S(1)} %collective-permute-done.14.refs_8_) | copy-start | bytes 3145732
  217.2 2.7 %collective-permute-start.23 = (f32[512,512]{1,0:T(8,128)S(1)}, f32[512,512]{1,0:T(8,128)S(1)}, u32[]{:S(2)}, u32[]{:S(2)}) collective-permute-start(f32[512,512]{1,0:T(8,128)S(1)} %collective-permute-done.14.refs_8_), channel_id=1, source_target_pairs={{0,1},{1,0},{2,3},{3,2},{4,5},{5,4},{6,7},{7,6},{8,9},{9,8},{10,11... | collective-permute-start | bytes 3145736 | tf_op jit(solution)/shard_map/ppermute | solution.py:185
  217.7 2.3 copy-start.6
  220.0 1.0 copy-start.7
